TPU v7x, 512 devices: a whole 4x8x8 slice. The times are simulated.
512 devices in a mesh: dp: 64 (over z_hi, y, core), rows: 8 (over z_lo, x).
Axes of the slice: x: 4, y: 8, z: 8 (z_hi: 4, z_lo: 2; z = z_hi * 2 + z_lo), core: 2. Of those that a mesh axis runs over, the one named last changes fastest.
Arguments:
- latents: bfloat16 [64, 32, 32, 640], P('dp', 'rows'), may hold values from -6 to 6
- target: bfloat16 [64, 32, 32, 640], P('dp', 'rows'), may hold values from -6 to 6
- weight: float32 [9, 640, 640], P(None, 'rows', 'dp'), may hold values from -0.078125 to 0.078125
- moment1: float32 [9, 640, 640], P(None, 'rows', 'dp'), may hold values from -6 to 6
- moment2: float32 [9, 640, 640], P(None, 'rows', 'dp'), may hold values from 0.5 to 4
Outputs:
- student: bfloat16 [64, 32, 32, 640], P('dp', 'rows')
- input_grad: bfloat16 [64, 32, 32, 640], P('dp', 'rows')
- new_weight: float32 [9, 640, 640], P(None, 'rows', 'dp')
- new_moment1: float32 [9, 640, 640], P(None, 'rows', 'dp')
- new_moment2: float32 [9, 640, 640], P(None, 'rows', 'dp')
All inputs are finite; a program needn't handle non-finite values.
Results may differ from a plain program's by a relative error of at most 0.009.
Values may be sent and summed in bfloat16 or wider, within the bound.
A program may use at most 128 MiB of HBM per device.

v0:
```python
import jax
import jax.numpy as jnp
from jax import lax
from jax.sharding import PartitionSpec as P


def sent_to_all(value, axis):
    copies = jnp.broadcast_to(value, (lax.axis_size(axis), *value.shape))
    return lax.all_to_all(copies, axis, split_axis=0, concat_axis=0, tiled=True)


def joined_along(tiles, dim):
    tiles = jnp.moveaxis(tiles, 0, dim)
    dims = tiles.shape
    return tiles.reshape(*dims[:dim], dims[dim] * dims[dim + 1], *dims[dim + 2 :])


def gather_directly(value, axis, dim):
    tiles = sent_to_all(value, axis)
    return joined_along(tiles, dim)


def padded_2(cells, sides, width):
    for axis, dim in sides:
        count = lax.axis_size(axis)
        ends = count - 1
        head = lax.slice_in_dim(cells, 0, width, axis=dim)
        tail = lax.slice_in_dim(cells, cells.shape[dim] - width, cells.shape[dim], axis=dim)
        cells = jnp.concatenate(
            [
                lax.ppermute(tail, axis, [(i, (i + 1) % count) for i in range(ends)]),
                cells,
                lax.ppermute(head, axis, [((i + 1) % count, i) for i in range(ends)]),
            ],
            axis=dim,
        )
    return cells


def cut_along(value, dim, length):
    dims = value.shape
    tiles = value.reshape(*dims[:dim], length, dims[dim] // length, *dims[dim + 1 :])
    return jnp.moveaxis(tiles, dim, 0)


def sum_at_owner(value, axis, dim):
    length = lax.axis_size(axis)
    tiles = lax.all_to_all(cut_along(value, dim, length), axis, 0, 0, tiled=True)
    return jnp.sum(tiles.astype(jnp.float32), axis=0)


def summed_on_arrival(value, axis, dim):
    length = lax.axis_size(axis)
    tiles = lax.all_to_all(cut_along(value, dim, length), axis, 0, 0, tiled=True)
    return jnp.sum(tiles, axis=0)


def forward_cells(padded, kernel, band, width):
    total = None
    for tap in range(9):
        a, c = divmod(tap, 3)
        term = jnp.einsum(
            "bhwc,cn->bhwn",
            padded[:, a : a + band, c : c + width],
            kernel[tap],
            preferred_element_type=jnp.float32,
        )
        total = term if total is None else total + term
    return total


def backward_cells(error_pad, kernel, band, width):
    total = None
    for tap in range(9):
        a, c = divmod(tap, 3)
        window = error_pad[:, 2 - a : 2 - a + band, 2 - c : 2 - c + width]
        term = jnp.einsum("bhwn,cn->bhwc", window, kernel[tap], preferred_element_type=jnp.float32)
        total = term if total is None else total + term
    return total


def band_partial(padded, error, band, width):
    pieces = []
    for tap in range(9):
        a, c = divmod(tap, 3)
        window = padded[:, a : a + band, c : c + width]
        pieces.append(
            jnp.einsum("bhwc,bhwn->cn", window, error, preferred_element_type=jnp.float32)
        )
    return lax.optimization_barrier(jnp.stack(pieces).astype(jnp.bfloat16)).astype(jnp.float32)


def per_device(latents, target, weight, moment1, moment2):
    band = latents.shape[1]
    width = latents.shape[2]
    side_pad = ((0, 0), (0, 0), (1, 1), (0, 0))
    kernel_part = gather_directly(weight.astype(jnp.bfloat16), "rows", 1)
    padded = padded_2(latents, (("rows", 1),), 1)
    padded = jnp.pad(padded, side_pad)
    kernel = lax.all_gather(kernel_part, "dp", axis=2, tiled=True)
    student = forward_cells(padded, kernel, band, width).astype(jnp.bfloat16)
    error = (student.astype(jnp.float32) - target.astype(jnp.float32)).astype(jnp.bfloat16)
    error_pad = padded_2(error, (("rows", 1),), 1)
    error_pad = jnp.pad(error_pad, side_pad)
    input_grad = backward_cells(error_pad, kernel, band, width).astype(jnp.bfloat16)
    partial_value = band_partial(padded, error, band, width)
    banded = sum_at_owner(partial_value.astype(jnp.bfloat16), "rows", 1)
    summed = summed_on_arrival(banded, "dp", 2)
    grad = summed / jnp.float32(latents.shape[0] * lax.axis_size("dp"))
    new_moment1 = 0.9 * moment1 + 0.1 * grad
    new_moment2 = 0.999 * moment2 + 0.001 * grad * grad
    new_weight = weight - 0.01 * new_moment1 / (jnp.sqrt(new_moment2) + 1e-08)
    return (student, input_grad, new_weight, new_moment1, new_moment2)


def solution(mesh):
    in_specs = (
        P("dp", "rows", None, None),
        P("dp", "rows", None, None),
        P(None, "rows", "dp"),
        P(None, "rows", "dp"),
        P(None, "rows", "dp"),
    )
    out_specs = (
        P("dp", "rows", None, None),
        P("dp", "rows", None, None),
        P(None, "rows", "dp"),
        P(None, "rows", "dp"),
        P(None, "rows", "dp"),
    )
    return jax.shard_map(
        per_device, mesh=mesh, in_specs=in_specs, out_specs=out_specs, check_vma=False
    )
```

profile of v0, /device:TPU:1, one launch (start us, length us, event | category | flops | bytes accessed | tf_op | source)
XLA Modules:
  0.0 417.5 jit_solution(13929723512859008652)
XLA Ops:
  8.5 11.8 %all_to_all.15 = bf16[8,2,3600]{2,1,0:T(2,128)(2,1)S(1)} all-to-all(bf16[8,2,3600]{2,1,0:T(2,128)(2,1)S(1)} %reshape.169), channel_id=1, replica_groups=mesh['dp'=64,'rows'=8] {'rows'}, dimensions={0} | all-to-all | bytes 230400 | tf_op jit(solution)/shard_map/all_to_all | solution.py:9
  23.7 4.0 collective-permute-start
  30.5 119.1 %all-gather.2.cloned.1.call-done = bf16[9,640,640]{1,0,2:T(8,128)(2,1)} async-done(((bf16[9,640,10]{1,0,2:T(8,128)(2,1)}), bf16[9,640,640]{1,0,2:T(8,128)(2,1)}) %all-gather.2.cloned.1.call-update) | async-done | bytes 7372816 | tf_op jit(solution)/shard_map/all_gather | solution.py:100
  149.6 27.1 %fusion.78 = (bf16[1,640,640]{1,0,2:T(2,128)(2,1)}, bf16[1,640,640]{1,0,2:T(2,128)(2,1)}, bf16[1,640,640]{1,0,2:T(2,128)(2,1)}, bf16[1,640,640]{1,0,2:T(2,128)(2...) fusion(bf16[9,640,640]{1,0,2:T(8,128)(2,1)} %all-gather.2.clone, ...), kind=kLoop, calls=%fused_computation.123 | loop fusion | bytes 14745600 | tf_op jit(solution)/shard_map/slice | solution.py:65
  176.7 3.5 copy.57
  180.2 3.7 copy.49
  188.1 4.2 %copy.50 = bf16[1,640,640]{2,1,0:T(8,128)(2,1)} copy(bf16[1,640,640]{1,0,2:T(2,128)(2,1)} %get-tuple-element.14) | data formatting | bytes 1638400
  192.3 4.2 %copy.51 = bf16[1,640,640]{2,1,0:T(8,128)(2,1)} copy(bf16[1,640,640]{1,0,2:T(2,128)(2,1)} %get-tuple-element.13) | data formatting | bytes 1638400
  196.6 3.2 copy.52
  199.8 3.5 copy.53
  203.3 3.7 copy.54
  207.1 3.7 copy.55
  210.8 3.7 copy.56
  225.6 2.9 copy-done
  228.5 3.7 copy.60
  232.3 87.8 %all_to_all.16 = bf16[8,9,80,640]{3,2,1,0:T(8,128)(2,1)S(1)} all-to-all(bf16[8,9,80,640]{3,2,1,0:T(8,128)(2,1)S(1)} %bitcast.259), channel_id=1, replica_groups=mesh['dp'=64,'rows'=8] {'rows'}, dimensions={0} | all-to-all | bytes 14745600 | tf_op jit(solution)/shard_map/all_to_all | solution.py:48
  327.5 4.8 %copy_bitcast_fusion.1 = f32[64,9,10,80]{3,2,1,0:T(8,128)} fusion(f32[9,80,64,10]{1,3,2,0:T(8,128)} %reshape.149), kind=kLoop, calls=%fused_computation.127 | loop fusion | bytes 3686400
  332.3 6.2 %reshape.171 = f32[64,1,7200]{2,1,0:T(1,128)} reshape(f32[64,9,10,80]{3,2,1,0:T(8,128)} %copy_bitcast_fusion.1) | data formatting | bytes 3686400
  338.6 8.3 %all-to-all-start.2 = ((f32[64,1,7200]{2,1,0:T(1,128)}), f32[64,1,7200]{2,1,0:T(1,128)S(1)}, u32[]{:S(2)}, u32[]{:S(2)}) async-start(f32[64,1,7200]{2,1,0:T(1,128)} %reshape.171), calls=%async_computation.2 | async-start | bytes 3735552 | tf_op jit(solution)/shard_map/all_to_all | solution.py:54
  349.2 4.0 collective-permute-start.2
  361.9 33.0 %all-to-all-done.2 = f32[64,1,7200]{2,1,0:T(1,128)S(1)} async-done(((f32[64,1,7200]{2,1,0:T(1,128)}), f32[64,1,7200]{2,1,0:T(1,128)S(1)}, u32[]{:S(2)}, u32[]{:S(2)}) %all-to-all-start.2) | async-done | bytes 1843232 | tf_op jit(solution)/shard_map/all_to_all | solution.py:54
  395.4 6.9 %reduce = f32[64,7200]{1,0:T(8,128)} reduce(f32[64,1,7200]{2,1,0:T(1,128)S(1)} %all-to-all-done.2, f32[]{:T(128)} %broadcast.31), dimensions={1}, to_apply=%all_to_all.11.reduce_sub_computation | reduce | bytes 3686404 | tf_op jit(solution)/shard_map/all_to_all | solution.py:54
  402.3 5.0 %reshape.172 = f32[64,9,10,80]{3,2,1,0:T(8,128)} reshape(f32[64,7200]{1,0:T(8,128)} %reduce) | data formatting | bytes 3686400
  407.3 2.7 bitcast_reduce_fusion
  (96 shorter events, 42.0 us)
Async XLA Ops:
  7.2 142.4 %all-gather.2.cloned.1.call-start = ((), (), s32[]{:S(2)}) async-start(), calls=%async_computation.3 | async-start | bytes 13312000 | tf_op jit(solution)/shard_map/all_gather | solution.py:100
  22.4 5.3 %collective-permute-start.1 = (bf16[1,1,32,640]{3,2,1,0:T(8,128)(2,1)S(1)}, bf16[1,1,32,640]{3,2,1,0:T(8,128)(2,1)S(1)}, u32[]{:S(2)}, u32[]{:S(2)}) collective-permute-start(bf16[1,1,32,640]{3,2,1,0:T(8,128)(2,1)S(1)} %get-tuple-element.20), channel_id=1, source_target_pairs={{1,0},{2,1},{3,2},{4,3},{5,4},{6,5},{7,6},{9,8},{10,9},{11,10},{12... | collective-permute-start | bytes 122888 | tf_op jit(solution)/shard_map/ppermute | solution.py:33
  23.7 5.1 %collective-permute-start = (bf16[1,1,32,640]{3,2,1,0:T(8,128)(2,1)S(1)}, bf16[1,1,32,640]{3,2,1,0:T(8,128)(2,1)S(1)}, u32[]{:S(2)}, u32[]{:S(2)}) collective-permute-start(bf16[1,1,32,640]{3,2,1,0:T(8,128)(2,1)S(1)} %get-tuple-element.19), channel_id=1, source_target_pairs={{0,1},{1,2},{2,3},{3,4},{4,5},{5,6},{6,7},{8,9},{9,10},{10,11},{11... | collective-permute-start | bytes 122888 | tf_op jit(solution)/shard_map/ppermute | solution.py:31
  180.2 16.4 %copy-start.10 = (bf16[1,640,640]{2,1,0:T(8,128)(2,1)}, bf16[1,640,640]{2,1,0:T(8,128)(2,1)S(1)}, u32[]{:S(2)}) copy-start(bf16[1,640,640]{2,1,0:T(8,128)(2,1)S(1)} %copy.57) | copy-start | bytes 2457604
  183.9 15.9 %copy-start.12 = (bf16[1,640,640]{2,1,0:T(8,128)(2,1)}, bf16[1,640,640]{2,1,0:T(8,128)(2,1)S(1)}, u32[]{:S(2)}) copy-start(bf16[1,640,640]{2,1,0:T(8,128)(2,1)S(1)} %copy.49) | copy-start | bytes 2457604
  199.8 14.8 %copy-start.17 = (bf16[1,4,32,640]{3,2,1,0:T(8,128)(2,1)S(1)}, bf16[1,4,32,640]{3,2,1,0:T(8,128)(2,1)}, u32[]{:S(2)}) copy-start(bf16[1,4,32,640]{3,2,1,0:T(8,128)(2,1)} %param.5) | copy-start | bytes 491524
  203.3 16.3 %copy-start.7 = (bf16[1,640,640]{2,1,0:T(8,128)(2,1)}, bf16[1,640,640]{2,1,0:T(8,128)(2,1)S(1)}, u32[]{:S(2)}) copy-start(bf16[1,640,640]{2,1,0:T(8,128)(2,1)S(1)} %copy.53) | copy-start | bytes 2457604
  207.1 12.9 %copy-start.5 = (bf16[1,640,640]{2,1,0:T(8,128)(2,1)}, bf16[1,640,640]{2,1,0:T(8,128)(2,1)S(1)}, u32[]{:S(2)}) copy-start(bf16[1,640,640]{2,1,0:T(8,128)(2,1)S(1)} %copy.54) | copy-start | bytes 2457604
  210.8 9.5 %copy-start.3 = (bf16[1,640,640]{2,1,0:T(8,128)(2,1)}, bf16[1,640,640]{2,1,0:T(8,128)(2,1)S(1)}, u32[]{:S(2)}) copy-start(bf16[1,640,640]{2,1,0:T(8,128)(2,1)S(1)} %copy.55) | copy-start | bytes 2457604
  214.5 6.0 %copy-start.1 = (bf16[1,640,640]{2,1,0:T(8,128)(2,1)}, bf16[1,640,640]{2,1,0:T(8,128)(2,1)S(1)}, u32[]{:S(2)}) copy-start(bf16[1,640,640]{2,1,0:T(8,128)(2,1)S(1)} %copy.56) | copy-start | bytes 2457604
  214.6 5.4 %copy-start.16 = (bf16[1,6,34,640]{3,2,1,0:T(8,128)(2,1)S(1)}, bf16[1,6,34,640]{3,2,1,0:T(8,128)(2,1)}, u32[]{:S(2)}) copy-start(bf16[1,6,34,640]{3,2,1,0:T(8,128)(2,1)} %select_maximum_fusion.2) | copy-start | bytes 783364
  214.6 6.0 %copy-start.18 = (f32[4,32,640]{2,1,0:T(8,128)S(1)}, f32[4,32,640]{2,1,0:T(8,128)}, u32[]{:S(2)}) copy-start(f32[4,32,640]{2,1,0:T(8,128)} %fusion.26) | copy-start | bytes 983044
  214.6 6.0 %copy-start.20 = (bf16[1,4,32,640]{3,2,1,0:T(8,128)(2,1)S(1)}, bf16[1,4,32,640]{3,2,1,0:T(8,128)(2,1)}, u32[]{:S(2)}) copy-start(bf16[1,4,32,640]{3,2,1,0:T(8,128)(2,1)} %param.6) | copy-start | bytes 491524
  332.3 22.9 %copy-start.11 = (bf16[1,640,640]{2,1,0:T(8,128)(2,1)S(1)}, bf16[1,640,640]{2,1,0:T(8,128)(2,1)}, u32[]{:S(2)}) copy-start(bf16[1,640,640]{2,1,0:T(8,128)(2,1)} %copy-done.10) | copy-start | bytes 2457604
  338.6 20.7 %copy-start.9 = (bf16[1,640,640]{2,1,0:T(8,128)(2,1)S(1)}, bf16[1,640,640]{2,1,0:T(8,128)(2,1)}, u32[]{:S(2)}) copy-start(bf16[1,640,640]{2,1,0:T(8,128)(2,1)} %copy.52) | copy-start | bytes 2457604
  338.6 56.3 %all-to-all-start.2 = ((f32[64,1,7200]{2,1,0:T(1,128)}), f32[64,1,7200]{2,1,0:T(1,128)S(1)}, u32[]{:S(2)}, u32[]{:S(2)}) async-start(f32[64,1,7200]{2,1,0:T(1,128)} %reshape.171), calls=%async_computation.2 | async-start | bytes 3735552 | tf_op jit(solution)/shard_map/all_to_all | solution.py:54
  346.9 12.0 %copy-start.13 = (bf16[1,640,640]{2,1,0:T(8,128)(2,1)S(1)}, bf16[1,640,640]{2,1,0:T(8,128)(2,1)}, u32[]{:S(2)}) copy-start(bf16[1,640,640]{2,1,0:T(8,128)(2,1)} %copy.51) | copy-start | bytes 2457604
  346.9 12.8 %copy-start.8 = (bf16[1,640,640]{2,1,0:T(8,128)(2,1)S(1)}, bf16[1,640,640]{2,1,0:T(8,128)(2,1)}, u32[]{:S(2)}) copy-start(bf16[1,640,640]{2,1,0:T(8,128)(2,1)} %copy-done.7) | copy-start | bytes 2457604
  346.9 12.8 %copy-start.15 = (bf16[1,4,32,640]{3,2,1,0:T(8,128)(2,1)S(1)}, bf16[1,4,32,640]{3,2,1,0:T(8,128)(2,1)}, u32[]{:S(2)}) copy-start(bf16[1,4,32,640]{3,2,1,0:T(8,128)(2,1)} %copy-done.14) | copy-start | bytes 491524
  347.9 5.3 %collective-permute-start.3 = (bf16[1,1,32,640]{3,2,1,0:T(8,128)(2,1)S(1)}, bf16[1,1,32,640]{3,2,1,0:T(8,128)(2,1)S(1)}, u32[]{:S(2)}, u32[]{:S(2)}) collective-permute-start(bf16[1,1,32,640]{3,2,1,0:T(8,128)(2,1)S(1)} %get-tuple-element.18), channel_id=1, source_target_pairs={{1,0},{2,1},{3,2},{4,3},{5,4},{6,5},{7,6},{9,8},{10,9},{11,10},{12... | collective-permute-start | bytes 122888 | tf_op jit(solution)/shard_map/ppermute | solution.py:33
  349.2 5.1 %collective-permute-start.2 = (bf16[1,1,32,640]{3,2,1,0:T(8,128)(2,1)S(1)}, bf16[1,1,32,640]{3,2,1,0:T(8,128)(2,1)S(1)}, u32[]{:S(2)}, u32[]{:S(2)}) collective-permute-start(bf16[1,1,32,640]{3,2,1,0:T(8,128)(2,1)S(1)} %get-tuple-element.17), channel_id=1, source_target_pairs={{0,1},{1,2},{2,3},{3,4},{4,5},{5,6},{6,7},{8,9},{9,10},{10,11},{11... | collective-permute-start | bytes 122888 | tf_op jit(solution)/shard_map/ppermute | solution.py:31
  402.3 7.7 %copy-start.19 = (f32[9,80,10]{1,2,0:T(8,128)S(1)}, f32[9,80,10]{1,2,0:T(8,128)}, u32[]{:S(2)}) copy-start(f32[9,80,10]{1,2,0:T(8,128)} %param.7) | copy-start | bytes 86404
  402.3 7.7 %copy-start.21 = (f32[9,80,10]{1,2,0:T(8,128)S(1)}, f32[9,80,10]{1,2,0:T(8,128)}, u32[]{:S(2)}) copy-start(f32[9,80,10]{1,2,0:T(8,128)} %param.8) | copy-start | bytes 86404
  402.3 7.7 %copy-start.22 = (f32[9,80,10]{1,2,0:T(8,128)S(1)}, f32[9,80,10]{1,2,0:T(8,128)}, u32[]{:S(2)}) copy-start(f32[9,80,10]{1,2,0:T(8,128)} %param.9) | copy-start | bytes 86404
  (5 other events, 19.6 us)
Sparse Core Ops, SparseCore 0:
  21.7 127.8 all-gather.1
where the time goes:
time: 421 us; the launch traced here: 418 us
  waiting for transfers between devices  154 us (37%)
  blocking collectives  99.6 us (24%)
  local copies, waits for them, and re-layouts  92.6 us (22%)
  matrix products  21.4 us (5%)
  starting transfers between devices  18.9 us (4%)
  other arithmetic  16.2 us (4%)
  between operations  14.6 us (3%)
    all_gather x1, waiting for transfers between devices, per_device(): kernel = lax.all_gather(kernel_part, 'dp', axis=2, tiled=True)  119 us
    all_to_all x1, blocking collectives, sum_at_owner(): lax.all_to_all(cut_along(value, dim, length), axis, 0, 0, tiled=True)  87.8 us
    unnamed x61, local copies, waits for them, and re-layouts  53.3 us
    all_to_all x1, waiting for transfers between devices, summed_on_arrival(): lax.all_to_all(cut_along(value, dim, length), axis, 0, 0, tiled=True)  33 us
    slice x1, local copies, waits for them, and re-layouts, forward_cells(): kernel[tap]  27.1 us
    all_to_all x1, blocking collectives, sent_to_all(): return lax.all_to_all(copies, axis, split_axis=0, concat_axis=0, tiled=True)  11.8 us
    dot_general x9, matrix products, forward_cells(): jnp.einsum('bhwc,cn->bhwn', padded[:, a:a + band, c:c + width], kernel[ta...  11.1 us
  transfers between devices with their start and end apart: 6, of which 4 were waited for; matrix products, arithmetic and copies ran while one was open for 3% of the time, Pallas kernels for 0%

commit v1 on v0

v1 whole, which is shorter than its diff:
```python
import jax
import jax.numpy as jnp
from jax import lax
from jax.sharding import PartitionSpec as P


def per_device(latents, target, weight, moment1, moment2):
    n_rows = lax.axis_size("rows")
    n_dp = lax.axis_size("dp")
    batch, band, width, ch = latents.shape
    taps, cs, ns = weight.shape
    height = band * n_rows
    cells = batch * band * width

    own = weight.astype(jnp.bfloat16).transpose(2, 0, 1).reshape(ns, taps * cs)
    kernel = lax.all_gather(own, "dp", axis=0, tiled=True)
    x = lax.all_to_all(latents, "rows", split_axis=3, concat_axis=1, tiled=True)
    pad = jnp.pad(x, ((0, 0), (1, 1), (1, 1), (0, 0)))
    wins = [pad[:, a : a + height, c : c + width] for a in range(3) for c in range(3)]
    x9 = jnp.concatenate(wins, axis=-1).reshape(batch * height * width, taps * cs)
    part = lax.dot_general(x9, kernel, (((1,), (1,)), ((), ())), preferred_element_type=jnp.float32)
    part = part.astype(jnp.bfloat16).reshape(batch, n_rows, band * width, ch)
    part = part.transpose(1, 0, 2, 3).reshape(n_rows, cells, ch)
    part = lax.all_to_all(part, "rows", 0, 0, tiled=True)
    student = jnp.sum(part.astype(jnp.float32), axis=0).astype(jnp.bfloat16)
    error = student.astype(jnp.float32) - target.reshape(cells, ch).astype(jnp.float32)
    error = error.astype(jnp.bfloat16).reshape(batch, band, width, ch)
    err = lax.all_gather(error, "rows", axis=1, tiled=True).reshape(-1, ch)
    grad = lax.dot_general(err, x9, (((0,), (0,)), ((), ())), preferred_element_type=jnp.float32)
    grad = grad.astype(jnp.bfloat16).reshape(n_dp, ns, taps * cs)
    grad = lax.all_to_all(grad, "dp", 0, 0, tiled=True)
    grad = jnp.sum(grad.astype(jnp.float32), axis=0) / jnp.float32(batch * n_dp)
    grad = grad.reshape(ns, taps, cs).transpose(1, 2, 0)
    back = jnp.dot(err, kernel, preferred_element_type=jnp.float32)
    back = back.reshape(batch, height, width, taps, cs)
    back = jnp.pad(back, ((0, 0), (1, 1), (1, 1), (0, 0), (0, 0)))
    total = None
    for tap in range(taps):
        a, c = divmod(tap, 3)
        term = back[:, 2 - a : 2 - a + height, 2 - c : 2 - c + width, tap]
        total = term if total is None else total + term
    input_grad = lax.all_to_all(
        total.astype(jnp.bfloat16), "rows", split_axis=1, concat_axis=3, tiled=True
    )
    new_moment1 = 0.9 * moment1 + 0.1 * grad
    new_moment2 = 0.999 * moment2 + 0.001 * grad * grad
    new_weight = weight - 0.01 * new_moment1 / (jnp.sqrt(new_moment2) + 1e-08)
    return (
        student.reshape(latents.shape),
        input_grad,
        new_weight,
        new_moment1,
        new_moment2,
    )


def solution(mesh):
    act = P("dp", "rows", None, None)
    par = P(None, "rows", "dp")
    return jax.shard_map(
        per_device,
        mesh=mesh,
        in_specs=(act, act, par, par, par),
        out_specs=(act, act, par, par, par),
        check_vma=False,
    )
```

time: 421 us -> 256 us (0.61)
  waiting for transfers between devices: 154 us -> 66.7 us
  local copies, waits for them, and re-layouts: 92.6 us -> 16 us
  blocking collectives: 99.6 us -> 116 us
  other arithmetic: 16.2 us -> 3.59 us
  matrix products: 21.4 us -> 8.98 us
  starting transfers between devices: 18.9 us -> 29.9 us
    all_gather x1, waiting for transfers between devices: 119 us -> 26.3 us  [per_device(): err = lax.all_gather(error, 'rows', axis=1, tiled=True).reshape(-1, ch)]
    all_gather x0 -> x1, blocking collectives: none -> 92.6 us  [per_device(): kernel = lax.all_gather(own, 'dp', axis=0, tiled=True)]
    all_to_all x2 -> x1, blocking collectives: 99.6 us -> 23 us  [per_device(): part = lax.all_to_all(part, 'rows', 0, 0, tiled=True)]
    unnamed x61 -> x42, local copies, waits for them, and re-layouts: 53.3 us -> 5.67 us
    slice x3 -> x1, local copies, waits for them, and re-layouts: 28.8 us -> 0.32 us  [per_device(): pad[:, a:a + height, c:c + width]]
    all_to_all x1 -> x3, starting transfers between devices: 8.33 us -> 29.9 us  [the longest x1 19.8 us: per_device(): grad = lax.all_to_all(grad, 'dp', 0, 0, tiled=True)]
    dot_general x27 -> x3, matrix products: 21.4 us -> 8.98 us  [the longest x1 3.48 us: per_device(): back = jnp.dot(err, kernel, preferred_element_type=jnp.float32)]
    ppermute x4 -> x0, starting transfers between devices: 10.5 us -> none  [the longest x2 7.98 us: padded_2(): lax.ppermute(tail, axis, [(i, (i + 1) % count) for i in range(ends)])]
  transfers between devices with their start and end apart: 6 -> 4, of which waited for: 4 -> 3; matrix products, arithmetic and copies ran while one was open for 3% -> 4% of each run, Pallas kernels for 0% -> 0%
where the time goes in v1:
time: 256 us; the launch traced here: 255 us
  blocking collectives  116 us (45%)
  waiting for transfers between devices  66.7 us (26%)
  starting transfers between devices  29.9 us (12%)
  local copies, waits for them, and re-layouts  16 us (6%)
  between operations  14.4 us (6%)
  matrix products  8.98 us (4%)
  other arithmetic  3.59 us (1%)
    all_gather x1, blocking collectives, per_device(): kernel = lax.all_gather(own, 'dp', axis=0, tiled=True)  92.6 us
    all_to_all x1, waiting for transfers between devices, per_device(): grad = lax.all_to_all(grad, 'dp', 0, 0, tiled=True)  39.4 us
    all_gather x1, waiting for transfers between devices, per_device(): err = lax.all_gather(error, 'rows', axis=1, tiled=True).reshape(-1, ch)  26.3 us
    all_to_all x1, blocking collectives, per_device(): part = lax.all_to_all(part, 'rows', 0, 0, tiled=True)  23 us
    all_to_all x1, starting transfers between devices, per_device(): grad = lax.all_to_all(grad, 'dp', 0, 0, tiled=True)  19.8 us
    all_to_all x1, starting transfers between devices, per_device(): x = lax.all_to_all(latents, 'rows', split_axis=3, concat_axis=1, tiled=True)  6.65 us
    unnamed x42, local copies, waits for them, and re-layouts  5.67 us
  transfers between devices with their start and end apart: 4, of which 3 were waited for; matrix products, arithmetic and copies ran while one was open for 4% of the time, Pallas kernels for 0%

profile of v1, /device:TPU:1, one launch (start us, length us, event | category | flops | bytes accessed | tf_op | source)
XLA Modules:
  0.0 255.2 jit_solution(7276642183336504303)
XLA Ops:
  7.2 1.3 copy.23
  8.5 1.3 reshape.187
  9.8 6.6 %all-to-all-start = ((bf16[8,2,5120]{2,1,0:T(2,128)(2,1)}), bf16[8,2,5120]{2,1,0:T(2,128)(2,1)S(1)}, u32[]{:S(2)}, u32[]{:S(2)}) async-start(bf16[8,2,5120]{2,1,0:T(2,128)(2,1)} %reshape.187), calls=%async_computation | async-start | bytes 327680 | tf_op jit(solution)/shard_map/all_to_all | solution.py:17
  16.6 92.6 %all-gather = bf16[64,10,720]{2,1,0:T(8,128)(2,1)S(1)} all-gather(bf16[1,10,720]{2,1,0:T(8,128)(2,1)S(1)} %reshape.181), channel_id=1, replica_groups=mesh['dp'=64,'rows'=8] {'dp'}, dimensions={0}, use_global_device_ids=true | all-gather | bytes 936000 | tf_op jit(solution)/shard_map/all_gather | solution.py:16
  110.9 2.4 concatenate.33
  113.3 2.8 %convolution_convert_fusion = bf16[1024,640]{1,0:T(8,128)(2,1)S(1)} fusion(bf16[1024,720]{1,0:T(8,128)(2,1)} %concatenate.33, bf16[640,720]{1,0:T(8,128)(2,1)S(1)} %reshape.182), kind=kOutput, calls=%fused_computation.11 | convolution fusion | flops 944373760 | bytes 3706880 | tf_op jit(solution)/shard_map/dot_general | solution.py:21
  116.2 23.0 %all_to_all.46 = bf16[8,128,640]{2,1,0:T(8,128)(2,1)S(1)} all-to-all(bf16[8,128,640]{2,1,0:T(8,128)(2,1)S(1)} %bitcast.78), channel_id=1, replica_groups=mesh['dp'=64,'rows'=8] {'rows'}, dimensions={0} | all-to-all | bytes 2621440 | tf_op jit(solution)/shard_map/all_to_all | solution.py:24
  139.4 1.7 subtract_convert_fusion
  141.2 1.3 copy.27
  142.6 2.4 concatenate.34
  145.0 26.3 %all-gather.3.cloned.1.call-done = bf16[1,32,32,640]{3,2,0,1:T(8,128)(2,1)} async-done(((bf16[1,4,32,640]{3,2,0,1:T(8,128)(2,1)}), bf16[1,32,32,640]{3,2,0,1:T(8,128)(2,1)}) %all-gather.3.cloned.1.call-update) | async-done | bytes 1310736 | tf_op jit(solution)/shard_map/all_gather | solution.py:28
  171.3 3.5 %convolution_bitcast_fusion = f32[1,32,32,9,80]{4,2,3,1,0:T(8,128)S(1)} fusion(bf16[9,80,640,1]{2,1,0,3:T(8,128)(2,1)S(1)} %bitcast.80, bf16[1,32,32,640]{3,2,0,1:T(8,128)(2,1)} %all-gather.3.cloned.1.call-done), kind=kOutput, calls=%fused_computation.9 | convolution fusion | flops 943718400 | bytes 5181440 | tf_op jit(solution)/shard_map/dot_general | solution.py:34
  174.8 1.3 fusion.15
  176.1 3.4 %all-to-all-start.2 = ((bf16[1,32,32,80]{3,2,0,1:T(8,128)(2,1)}), bf16[1,32,32,80]{3,2,0,1:T(8,128)(2,1)S(1)}, u32[]{:S(2)}, u32[]{:S(2)}) async-start(bf16[1,32,32,80]{3,2,0,1:T(8,128)(2,1)} %fusion.15), calls=%async_computation.2 | async-start | bytes 524288 | tf_op jit(solution)/shard_map/all_to_all | solution.py:42
  179.5 2.7 %bitcast_convert_fusion = bf16[640,720]{0,1:T(8,128)(2,1)S(1)} fusion(bf16[1,32,32,720]{3,2,1,0:T(8,128)(2,1)S(1)} %copy-done.10, bf16[1,32,32,640]{3,2,0,1:T(8,128)(2,1)} %all-gather.3.cloned.1.call-done), kind=kOutput, calls=%fused_computation.10 | convolution fusion | flops 944179200 | bytes 3706880 | tf_op jit(solution)/shard_map/dot_general | solution.py:29
  182.2 1.0 copy.31
  183.2 1.4 reshape.175
  184.6 1.0 all-to-all-done.2
  185.6 19.8 %all-to-all-start.3 = ((bf16[64,10,720]{2,1,0:T(8,128)(2,1)}), bf16[64,10,720]{2,1,0:T(8,128)(2,1)S(1)}, u32[]{:S(2)}, u32[]{:S(2)}) async-start(bf16[64,10,720]{2,1,0:T(8,128)(2,1)} %reshape.175), calls=%async_computation.3 | async-start | bytes 3145728 | tf_op jit(solution)/shard_map/all_to_all | solution.py:31
  205.6 0.9 all_to_all.40
  206.5 39.4 %all-to-all-done.3 = bf16[64,10,720]{2,1,0:T(8,128)(2,1)S(1)} async-done(((bf16[64,10,720]{2,1,0:T(8,128)(2,1)}), bf16[64,10,720]{2,1,0:T(8,128)(2,1)S(1)}, u32[]{:S(2)}, u32[]{:S(2)}) %all-to-all-start.3) | async-done | bytes 921632 | tf_op jit(solution)/shard_map/all_to_all | solution.py:31
  246.4 0.6 copy.35
  247.0 0.6 copy.36
  247.7 0.6 copy.37
  (50 shorter events, 2.7 us)
Async XLA Ops:
  7.2 9.3 %copy-start.13 = (f32[9,80,10]{1,2,0:T(8,128)S(1)}, f32[9,80,10]{1,2,0:T(8,128)}, u32[]{:S(2)}) copy-start(f32[9,80,10]{1,2,0:T(8,128)} %param.7) | copy-start | bytes 86404
  9.8 100.0 %all-to-all-start = ((bf16[8,2,5120]{2,1,0:T(2,128)(2,1)}), bf16[8,2,5120]{2,1,0:T(2,128)(2,1)S(1)}, u32[]{:S(2)}, u32[]{:S(2)}) async-start(bf16[8,2,5120]{2,1,0:T(2,128)(2,1)} %reshape.187), calls=%async_computation | async-start | bytes 327680 | tf_op jit(solution)/shard_map/all_to_all | solution.py:17
  16.4 154.8 %all-gather.3.cloned.1.call-start = ((), (), s32[]{:S(2)}) async-start(), calls=%async_computation.4 | async-start | bytes 1474560 | tf_op jit(solution)/shard_map/all_gather | solution.py:28
  110.8 2.5 copy-start
  110.8 2.5 copy-start.2
  110.8 2.5 copy-start.4
  110.8 2.5 copy-start.6
  110.9 2.5 copy-start.8
  139.4 5.6 %copy-start.12 = (bf16[128,640]{1,0:T(8,128)(2,1)}, bf16[128,640]{1,0:T(8,128)(2,1)S(1)}, u32[]{:S(2)}) copy-start(bf16[128,640]{1,0:T(8,128)(2,1)S(1)} %reduce_sum.21) | copy-start | bytes 491524
  139.4 3.1 %copy-start.1 = (bf16[1,32,32,80]{3,2,1,0:T(8,128)(2,1)S(1)}, bf16[1,32,32,80]{3,2,1,0:T(8,128)(2,1)}, u32[]{:S(2)}) copy-start(bf16[1,32,32,80]{3,2,1,0:T(8,128)(2,1)} %copy-done) | copy-start | bytes 491524
  139.4 3.1 %copy-start.3 = (bf16[1,32,32,80]{3,2,1,0:T(8,128)(2,1)S(1)}, bf16[1,32,32,80]{3,2,1,0:T(8,128)(2,1)}, u32[]{:S(2)}) copy-start(bf16[1,32,32,80]{3,2,1,0:T(8,128)(2,1)} %copy-done.2) | copy-start | bytes 491524
  139.4 3.1 %copy-start.5 = (bf16[1,32,32,80]{3,2,1,0:T(8,128)(2,1)S(1)}, bf16[1,32,32,80]{3,2,1,0:T(8,128)(2,1)}, u32[]{:S(2)}) copy-start(bf16[1,32,32,80]{3,2,1,0:T(8,128)(2,1)} %copy-done.4) | copy-start | bytes 491524
  139.4 3.1 %copy-start.7 = (bf16[1,32,32,80]{3,2,1,0:T(8,128)(2,1)S(1)}, bf16[1,32,32,80]{3,2,1,0:T(8,128)(2,1)}, u32[]{:S(2)}) copy-start(bf16[1,32,32,80]{3,2,1,0:T(8,128)(2,1)} %copy-done.6) | copy-start | bytes 491524
  139.4 3.1 %copy-start.9 = (bf16[1,32,32,80]{3,2,1,0:T(8,128)(2,1)S(1)}, bf16[1,32,32,80]{3,2,1,0:T(8,128)(2,1)}, u32[]{:S(2)}) copy-start(bf16[1,32,32,80]{3,2,1,0:T(8,128)(2,1)} %copy-done.8) | copy-start | bytes 491524
  142.6 28.7 %copy-start.11 = (bf16[720,640]{1,0:T(8,128)(2,1)S(1)}, bf16[720,640]{1,0:T(8,128)(2,1)}, u32[]{:S(2)}) copy-start(bf16[720,640]{1,0:T(8,128)(2,1)} %copy.27) | copy-start | bytes 2764804
  174.8 4.7 %copy-start.10 = (bf16[1,32,32,720]{3,2,1,0:T(8,128)(2,1)S(1)}, bf16[1,32,32,720]{3,2,1,0:T(8,128)(2,1)}, u32[]{:S(2)}) copy-start(bf16[1,32,32,720]{3,2,1,0:T(8,128)(2,1)} %concatenate.34) | copy-start | bytes 4423684
  176.1 9.5 %all-to-all-start.2 = ((bf16[1,32,32,80]{3,2,0,1:T(8,128)(2,1)}), bf16[1,32,32,80]{3,2,0,1:T(8,128)(2,1)S(1)}, u32[]{:S(2)}, u32[]{:S(2)}) async-start(bf16[1,32,32,80]{3,2,0,1:T(8,128)(2,1)} %fusion.15), calls=%async_computation.2 | async-start | bytes 524288 | tf_op jit(solution)/shard_map/all_to_all | solution.py:42
  185.6 60.3 %all-to-all-start.3 = ((bf16[64,10,720]{2,1,0:T(8,128)(2,1)}), bf16[64,10,720]{2,1,0:T(8,128)(2,1)S(1)}, u32[]{:S(2)}, u32[]{:S(2)}) async-start(bf16[64,10,720]{2,1,0:T(8,128)(2,1)} %reshape.175), calls=%async_computation.3 | async-start | bytes 3145728 | tf_op jit(solution)/shard_map/all_to_all | solution.py:31
  205.4 40.9 %copy-start.14 = (f32[9,80,10]{1,2,0:T(8,128)S(1)}, f32[9,80,10]{1,2,0:T(8,128)}, u32[]{:S(2)}) copy-start(f32[9,80,10]{1,2,0:T(8,128)} %param.7) | copy-start | bytes 86404
  205.4 40.9 %copy-start.15 = (f32[9,80,10]{1,2,0:T(8,128)S(1)}, f32[9,80,10]{1,2,0:T(8,128)}, u32[]{:S(2)}) copy-start(f32[9,80,10]{1,2,0:T(8,128)} %param.8) | copy-start | bytes 86404
  205.4 40.9 %copy-start.16 = (f32[9,80,10]{1,2,0:T(8,128)S(1)}, f32[9,80,10]{1,2,0:T(8,128)}, u32[]{:S(2)}) copy-start(f32[9,80,10]{1,2,0:T(8,128)} %param.9) | copy-start | bytes 86404
Sparse Core Ops, SparseCore 0:
  141.3 29.9 all-gather.2

commit v2 on v1

v2 whole, which is shorter than its diff:
```python
import jax
import jax.numpy as jnp
from jax import lax
from jax.experimental import pallas as pl
from jax.experimental.pallas import tpu as pltpu
from jax.sharding import PartitionSpec as P

MESH = pl.DeviceIdType.MESH
F32 = jnp.float32
BF16 = jnp.bfloat16
Y_ORDER = (1, 7, 2, 6, 3, 5, 4)
N_SEM = 128
NT = (((1,), (1,)), ((), ()))
TN = (((0,), (0,)), ((), ()))


def dot(a, b, dims=(((1,), (0,)), ((), ()))):
    return lax.dot_general(a, b, dims, preferred_element_type=F32)


def kernel(
    lat, tgt, wgt, stu_out, ig_out, g_out,
    kp, km, xs, st, sk, ts, tb, sb, rb, e3, gacc, ga, ra, rs, rd, ysend, yr, zs, zr,
    igp, igr, igc, ia, isum, idr, send_sem, recv_sem,
):
    dp, row = lax.axis_index("dp"), lax.axis_index("rows")
    k, y, zh = dp % 2, (dp // 2) % 8, dp // 16
    x, zl = row % 4, row // 4

    def dev(dz=0, dy=0, flip=False, dx=0, flip_zl=False):
        core = 1 - k if flip else k
        low = 1 - zl if flip_zl else zl
        return (((zh + dz) % 4 * 8 + (y + dy) % 8) * 2 + core, low * 4 + (x + dx) % 4)

    def row_dev(dr):
        return (dp, (row + dr) % 8)

    copies = []

    def send(src, dst, device):
        i = len(copies)
        copy = pltpu.make_async_remote_copy(
            src_ref=src,
            dst_ref=dst,
            send_sem=send_sem.at[i],
            recv_sem=recv_sem.at[i],
            device_id=device,
            device_id_type=MESH,
        )
        copy.start()
        copies.append(copy)
        return copy

    def lanes(j):
        return pl.ds(pl.multiple_of(j * 128, 128), 128)

    pieces = [wgt[t] for t in range(9)] + [jnp.zeros((80, 38), F32)]
    kp[x, zl, :, lanes(y)] = jnp.concatenate(pieces, axis=1).astype(BF16)
    own = kp.at[x, zl, :, lanes(y)]
    p0 = send(own, own, dev(flip_zl=True))
    up0 = send(lat.at[0:64], xs.at[3, 32:96], dev(dz=1))
    dn1 = send(lat.at[64:128], xs.at[1, 96:160], dev(dz=-1))
    up1 = send(lat.at[64:128], xs.at[3, 96:160], dev(dz=1))
    dn0 = send(lat.at[0:64], xs.at[1, 32:96], dev(dz=-1))
    part = [send(lat, xs.at[4, 32:160], dev(flip=True))]
    top = [send(lat.at[0:32], xs.at[0, 160:192], row_dev(-1))]
    bot = [send(lat.at[96:128], xs.at[0, 0:32], row_dev(1))]
    xs[0, 32:160] = lat[...]

    p0.wait_recv()
    block = kp.at[x, :, :, lanes(y)]
    p1 = {dy: send(block, block, dev(dy=dy)) for dy in Y_ORDER}
    right, left, fwd_r, fwd_l = {}, {}, {}, {}
    right[0] = send(block, block, dev(dx=1))
    left[0] = send(block, block, dev(dx=-1))

    lane = lax.broadcasted_iota(jnp.int32, (640, 128), 1)
    chan = lax.broadcasted_iota(jnp.int32, (640, 128), 0)
    place = lane + 10 * ((lane * 205) >> 11)
    for s in range(8):
        core = k if s < 4 else 1 - k
        hit = (chan == place + (zh + s % 4) % 4 * 160 + core * 10) & (lane < 80)
        st[:, s * 128 : s * 128 + 128] = jnp.where(hit, 1.0, 0.0).astype(BF16)

    def halos(s):
        top.append(send(xs.at[s, 32:64], xs.at[s, 160:192], row_dev(-1)))
        bot.append(send(xs.at[s, 128:160], xs.at[s, 0:32], row_dev(1)))

    up0.wait_recv()
    over0 = send(xs.at[3, 32:96], xs.at[2, 32:96], dev(dz=1))
    dn1.wait_recv()
    over1 = send(xs.at[1, 96:160], xs.at[2, 96:160], dev(dz=-1))

    def y_step(dy):
        p1[dy].wait_recv()
        got = kp.at[x, :, :, lanes((y - dy) % 8)]
        right[dy] = send(got, got, dev(dx=1))
        left[dy] = send(got, got, dev(dx=-1))

    def x_step(dy):
        right[dy].wait_recv()
        got = kp.at[(x + 3) % 4, 0, :, lanes((y - dy) % 8)]
        fwd_r[dy] = send(got, got, dev(dx=1))
        left[dy].wait_recv()
        got = kp.at[(x + 1) % 4, 1, :, lanes((y - dy) % 8)]
        fwd_l[dy] = send(got, got, dev(dx=-1))

    y_step(1)
    y_step(7)
    x_step(0)
    up1.wait_recv()
    halos(3)
    part.append(send(xs.at[3, 32:160], xs.at[7, 32:160], dev(flip=True)))
    dn0.wait_recv()
    halos(1)
    part.append(send(xs.at[1, 32:160], xs.at[5, 32:160], dev(flip=True)))
    y_step(2)
    y_step(6)
    x_step(1)
    x_step(7)

    ts[...] = dot(tgt[...], st[...]).astype(BF16)
    tsent = []
    for s in (4, 1, 3, 5, 7, 2, 6):
        back = s // 4 * 4 + (-s) % 4
        src = ts.at[:, s * 128 : s * 128 + 128]
        tsent.append(send(src, tb.at[back], dev(dz=s % 4, flip=s >= 4)))
    tb[0] = ts[:, 0:128]

    y_step(3)
    y_step(5)
    y_step(4)
    x_step(2)
    x_step(6)
    over0.wait_recv()
    over1.wait_recv()
    halos(2)
    part.append(send(xs.at[2, 32:160], xs.at[6, 32:160], dev(flip=True)))
    x_step(3)
    x_step(5)
    x_step(4)

    l0 = lax.broadcasted_iota(jnp.int32, (128, 768), 0)
    q = lax.broadcasted_iota(jnp.int32, (128, 768), 1)
    tap = (l0 * 205) >> 11
    third = (tap * 11) >> 5
    want = third * 256 + (tap - 3 * third) * 80 + l0 - 10 * tap
    diff = jnp.where(l0 < 90, q - want, -1)

    def make_sk(j, carry):
        hit = jnp.where(diff == j * 10, 1.0, 0.0)
        sk[pl.ds(pl.multiple_of(j * 128, 128), 128), :] = hit.astype(BF16)
        return carry

    lax.fori_loop(0, 8, make_sk, 0)

    def place_kernel(dx):
        at = (x + dx) % 4
        out = dot(kp[at].reshape(160, 1024), sk[...]).astype(BF16)
        km[pl.ds(pl.multiple_of(at * 80, 16), 80), :] = out[:80]
        km[pl.ds(pl.multiple_of(320 + at * 80, 16), 80), :] = out[80:]

    place_kernel(0)
    place_kernel(1)
    place_kernel(3)

    for c in top + bot:
        c.wait_recv()
    part.append(send(xs.at[0:4, 0:32], xs.at[4:8, 0:32], dev(flip=True)))
    part.append(send(xs.at[0:4, 160:192], xs.at[4:8, 160:192], dev(flip=True)))
    for dy in (0,) + Y_ORDER:
        fwd_r[dy].wait_recv()
        fwd_l[dy].wait_recv()
    place_kernel(2)
    for c in part:
        c.wait_recv()
    part[-1].wait_send()
    part[-2].wait_send()

    @pl.when(row == 0)
    def _():
        xs[:, 0:32, :] = jnp.zeros((8, 32, 640), BF16)

    @pl.when(row == 7)
    def _():
        xs[:, 160:192, :] = jnp.zeros((8, 32, 640), BF16)

    for c in tsent:
        c.wait_recv()

    col = lax.broadcasted_iota(jnp.int32, (256, 128), 0) % 32
    first, last = col == 0, col == 31
    real = lax.broadcasted_iota(jnp.int32, (256, 128), 1) < 80

    def forward(m, carry):
        two = pl.ds(2 * m, 2)
        acc = None
        for a in range(3):
            win = xs[two, 32 * a : 32 * a + 128, :].reshape(256, 640)
            term = dot(win, km[:, 256 * a : 256 * a + 256])
            acc = term if acc is None else acc + term
        mid = pltpu.roll(acc, 176, 1)[:, :128]
        end = pltpu.roll(acc, 96, 1)[:, :128]
        total = mid + jnp.where(first, 0.0, pltpu.roll(acc[:, :128], 1, 0))
        total = total + jnp.where(last, 0.0, pltpu.roll(end, 255, 0))
        stu = jnp.where(real, total, 0.0).astype(BF16)
        sb[two] = stu.reshape(2, 128, 128)
        err = stu.astype(F32) - tb[two].reshape(256, 128).astype(F32)
        err = err.astype(BF16).astype(F32)
        zero = jnp.zeros((256, 128), F32)
        nxt = jnp.where(last, 0.0, pltpu.roll(err, 255, 0))
        prv = jnp.where(first, 0.0, pltpu.roll(err, 1, 0))
        wide = jnp.concatenate([nxt, zero], axis=1)
        wide = wide + pltpu.roll(jnp.concatenate([err, zero], axis=1), 80, 1)
        wide = wide + pltpu.roll(jnp.concatenate([prv, zero], axis=1), 160, 1)
        e3[two, 32:160, :] = wide.astype(BF16).reshape(2, 128, 256)
        return carry

    lax.fori_loop(0, 4, forward, 0)

    etop = send(e3.at[:, 32:64], e3.at[:, 160:192], row_dev(-1))
    ebot = send(e3.at[:, 128:160], e3.at[:, 0:32], row_dev(1))
    ssent = []
    for s in (4, 1, 3, 5, 7, 2, 6):
        back = s // 4 * 4 + (-s) % 4
        dst = rb.at[:, back * 128 : back * 128 + 128]
        ssent.append(send(sb.at[s], dst, dev(dz=s % 4, flip=s >= 4)))
    rb[:, 0:128] = sb[0]

    gacc[...] = jnp.zeros((640, 768), F32)

    def weight_grad(m, carry):
        two = pl.ds(2 * m, 2)
        errs = e3[two, 32:160, :].reshape(256, 256)
        for a in range(3):
            win = xs[two, 32 * a : 32 * a + 128, :].reshape(256, 640)
            gacc[:, 256 * a : 256 * a + 256] += dot(win, errs, TN)
        return carry

    lax.fori_loop(0, 4, weight_grad, 0)

    def place_grad(dx):
        at = (x + dx) % 4
        low = gacc[pl.ds(pl.multiple_of(at * 80, 8), 80), :]
        high = gacc[pl.ds(pl.multiple_of(320 + at * 80, 8), 80), :]
        both = jnp.concatenate([low, high], axis=0).astype(BF16)
        ga[dx] = dot(both, sk[...], NT).astype(BF16).reshape(2, 80, 1024)

    place_grad(2)
    gr_a = send(ga.at[2, 0], ra.at[0], dev(dx=1))
    gr_b = send(ga.at[2, 1], ra.at[1], dev(dx=-1))
    place_grad(1)
    gd_a = send(ga.at[1, 1], rd.at[1], dev(dx=1))
    place_grad(3)
    gd_b = send(ga.at[3, 0], rd.at[0], dev(dx=-1))
    place_grad(0)

    etop.wait_recv()
    ebot.wait_recv()
    etop.wait_send()
    ebot.wait_send()

    @pl.when(row == 0)
    def _():
        e3[:, 0:32, :] = jnp.zeros((8, 32, 256), BF16)

    @pl.when(row == 7)
    def _():
        e3[:, 160:192, :] = jnp.zeros((8, 32, 256), BF16)

    def input_grad(m, carry):
        two = pl.ds(2 * m, 2)
        acc = None
        for a in range(3):
            win = e3[two, 64 - 32 * a : 192 - 32 * a, :].reshape(256, 256)
            term = dot(win, km[:, 256 * a : 256 * a + 256], NT)
            acc = term if acc is None else acc + term
        igp[two] = acc.astype(BF16).reshape(2, 128, 640)
        return carry

    lax.fori_loop(2, 4, input_grad, 0)
    ip = send(igp.at[4:8], igr, dev(flip=True))
    gr_a.wait_recv()
    rs[0] = (ra[0].astype(F32) + ga[1, 0].astype(F32)).astype(BF16)
    gs_a = send(rs.at[0], rd.at[2], dev(dx=1))
    gr_b.wait_recv()
    rs[1] = (ra[1].astype(F32) + ga[3, 1].astype(F32)).astype(BF16)
    gs_b = send(rs.at[1], rd.at[3], dev(dx=-1))
    lax.fori_loop(0, 2, input_grad, 0)
    ip.wait_recv()
    for s in (2, 1, 3, 0):
        igc[s] = (igp[s].astype(F32) + igr[s].astype(F32)).astype(BF16)
        if s == 2:
            ir_a = send(igc.at[2, 0:64], ia.at[0], dev(dz=1))
            ir_b = send(igc.at[2, 64:128], ia.at[1], dev(dz=-1))
        if s == 1:
            id_a = send(igc.at[1, 64:128], idr.at[1], dev(dz=1))
        if s == 3:
            id_b = send(igc.at[3, 0:64], idr.at[0], dev(dz=-1))

    for c in (gd_a, gd_b, gs_a, gs_b):
        c.wait_recv()
    low = ga[0, 0].astype(F32) + rd[0].astype(F32) + rd[2].astype(F32)
    high = ga[0, 1].astype(F32) + rd[1].astype(F32) + rd[3].astype(F32)
    ysend[0] = low.astype(BF16)
    ysend[1] = high.astype(BF16)
    ysent = []
    for i, dy in enumerate(Y_ORDER):
        src = ysend.at[:, :, lanes((y + dy) % 8)]
        ysent.append(send(src, yr.at[i], dev(dy=dy)))

    ir_a.wait_recv()
    isum[0] = (ia[0].astype(F32) + igc[1, 0:64].astype(F32)).astype(BF16)
    is_a = send(isum.at[0], idr.at[2], dev(dz=1))
    ir_b.wait_recv()
    isum[1] = (ia[1].astype(F32) + igc[3, 64:128].astype(F32)).astype(BF16)
    is_b = send(isum.at[1], idr.at[3], dev(dz=-1))

    for c in ssent:
        c.wait_recv()
    stu_out[...] = dot(rb[...], st[...], NT).astype(BF16)

    total = ysend[:, :, lanes(y)].astype(F32)
    for i in range(7):
        ysent[i].wait_recv()
        total = total + yr[i].astype(F32)
    zs[...] = total
    zc = send(zs.at[1 - zl], zr, dev(flip_zl=True))

    for c in (id_a, id_b, is_a, is_b):
        c.wait_recv()
    low = igc[0, 0:64].astype(F32) + idr[0].astype(F32) + idr[2].astype(F32)
    high = igc[0, 64:128].astype(F32) + idr[1].astype(F32) + idr[3].astype(F32)
    ig_out[0:64] = low.astype(BF16)
    ig_out[64:128] = high.astype(BF16)

    zc.wait_recv()
    grad = (zs[zl] + zr[...]) * (1.0 / 64.0)
    for t in range(9):
        g_out[t] = grad[:, 10 * t : 10 * t + 10]
    waited = (part[-1], part[-2], etop, ebot)
    for c in copies:
        if not any(c is w for w in waited):
            c.wait_send()


def per_device(latents, target, weight, moment1, moment2):
    vmem = pl.BlockSpec(memory_space=pltpu.VMEM)
    student, input_grad, grad = pl.pallas_call(
        kernel,
        out_shape=(
            jax.ShapeDtypeStruct((128, 640), BF16),
            jax.ShapeDtypeStruct((128, 640), BF16),
            jax.ShapeDtypeStruct((9, 80, 10), F32),
        ),
        in_specs=[vmem] * 3,
        out_specs=(vmem,) * 3,
        scratch_shapes=[
            pltpu.VMEM((4, 2, 80, 1024), BF16),
            pltpu.VMEM((640, 768), BF16),
            pltpu.VMEM((8, 192, 640), BF16),
            pltpu.VMEM((640, 1024), BF16),
            pltpu.VMEM((1024, 768), BF16),
            pltpu.VMEM((128, 1024), BF16),
            pltpu.VMEM((8, 128, 128), BF16),
            pltpu.VMEM((8, 128, 128), BF16),
            pltpu.VMEM((128, 1024), BF16),
            pltpu.VMEM((8, 192, 256), BF16),
            pltpu.VMEM((640, 768), F32),
            pltpu.VMEM((4, 2, 80, 1024), BF16),
            pltpu.VMEM((2, 80, 1024), BF16),
            pltpu.VMEM((2, 80, 1024), BF16),
            pltpu.VMEM((4, 80, 1024), BF16),
            pltpu.VMEM((2, 80, 1024), BF16),
            pltpu.VMEM((7, 2, 80, 128), BF16),
            pltpu.VMEM((2, 80, 128), F32),
            pltpu.VMEM((80, 128), F32),
            pltpu.VMEM((8, 128, 640), BF16),
            pltpu.VMEM((4, 128, 640), BF16),
            pltpu.VMEM((4, 128, 640), BF16),
            pltpu.VMEM((2, 64, 640), BF16),
            pltpu.VMEM((2, 64, 640), BF16),
            pltpu.VMEM((4, 64, 640), BF16),
            pltpu.SemaphoreType.DMA((N_SEM,)),
            pltpu.SemaphoreType.DMA((N_SEM,)),
        ],
        compiler_params=pltpu.CompilerParams(has_side_effects=True, vmem_limit_bytes=48 << 20),
    )(latents.reshape(128, 640), target.reshape(128, 640), weight)
    new_moment1 = 0.9 * moment1 + 0.1 * grad
    new_moment2 = 0.999 * moment2 + 0.001 * grad * grad
    new_weight = weight - 0.01 * new_moment1 / (jnp.sqrt(new_moment2) + 1e-08)
    return (
        student.reshape(latents.shape),
        input_grad.reshape(latents.shape),
        new_weight,
        new_moment1,
        new_moment2,
    )


def solution(mesh):
    act = P("dp", "rows", None, None)
    par = P(None, "rows", "dp")
    return jax.shard_map(
        per_device,
        mesh=mesh,
        in_specs=(act, act, par, par, par),
        out_specs=(act, act, par, par, par),
        check_vma=False,
    )
```

time: 256 us -> 94.8 us (0.37)
  blocking collectives: 116 us -> 0 us
  Pallas kernels: 0 us -> 86.9 us
  waiting for transfers between devices: 66.7 us -> 0 us
  starting transfers between devices: 29.9 us -> 0 us
  between operations: 14.4 us -> 0.73 us
  local copies, waits for them, and re-layouts: 16 us -> 5.9 us
  matrix products: 8.98 us -> 0 us
  other arithmetic: 3.59 us -> 0.26 us
    all_gather x1 -> x0, blocking collectives: 92.6 us -> none  [per_device(): kernel = lax.all_gather(own, 'dp', axis=0, tiled=True)]
    pallas_call x0 -> x1, Pallas kernels: none -> 86.9 us  [per_device(): pl.pallas_call(kernel, out_shape=(jax.ShapeDtypeStruct((128, 640), BF16),...]
    all_to_all x3 -> x0, waiting for transfers between devices: 40.4 us -> none  [the longest x1 39.4 us: per_device(): grad = lax.all_to_all(grad, 'dp', 0, 0, tiled=True)]
    all_to_all x3 -> x0, starting transfers between devices: 29.9 us -> none  [the longest x1 19.8 us: per_device(): grad = lax.all_to_all(grad, 'dp', 0, 0, tiled=True)]
    all_gather x1 -> x0, waiting for transfers between devices: 26.3 us -> none  [per_device(): err = lax.all_gather(error, 'rows', axis=1, tiled=True).reshape(-1, ch)]
    all_to_all x1 -> x0, blocking collectives: 23 us -> none  [per_device(): part = lax.all_to_all(part, 'rows', 0, 0, tiled=True)]
    dot_general x3 -> x0, matrix products: 8.98 us -> none  [the longest x1 3.48 us: per_device(): back = jnp.dot(err, kernel, preferred_element_type=jnp.float32)]
    concatenate x2 -> x0, local copies, waits for them, and re-layouts: 4.81 us -> none  [per_device(): jnp.concatenate(wins, axis=-1).reshape(batch * height * width, taps * cs)]
  transfers between devices with their start and end apart: 4 -> 0, of which waited for: 3 -> 0; matrix products, arithmetic and copies ran while one was open for 4% -> 0% of each run, Pallas kernels for 0% -> 0%
where the time goes in v2:
time: 94.8 us; the launch traced here: 93.8 us
  Pallas kernels  86.9 us (92%)
  local copies, waits for them, and re-layouts  5.9 us (6%)
    pallas_call x1, Pallas kernels, per_device(): pl.pallas_call(kernel, out_shape=(jax.ShapeDtypeStruct((128, 640), BF16),...  86.9 us
    unnamed x16, local copies, waits for them, and re-layouts  5.9 us

profile of v2, /device:TPU:1, one launch (start us, length us, event | category | flops | bytes accessed | tf_op | source)
XLA Modules:
  0.0 93.8 jit_solution(16878766456056262731)
XLA Ops:
  0.6 0.0 copy-start
  0.6 0.0 copy-start.1
  0.7 1.1 %copy.17.wgt = f32[9,80,10]{2,1,0:T(8,128)S(1)} copy(f32[9,80,10]{1,2,0:T(8,128)} %param.7) | data formatting | bytes 57600 | tf_op args[2]
  1.8 0.0 copy-done
  1.8 0.0 copy-done.1
  1.8 0.0 copy-start.2
  1.8 86.9 %shard_map.92 = (bf16[128,640]{1,0:T(8,128)(2,1)S(1)}, bf16[128,640]{1,0:T(8,128)(2,1)S(1)}, f32[9,80,10]{2,1,0:T(8,128)S(1)}) custom-call(bf16[128,640]{1,0:T(8,128)(2,1)S(1)} %bitcast.6, bf16[128,640]{1,0:T(8,128)(2,1)S(1)} %bitcast.7, f32[9,80,10]{2,1,0:T(8,128)S(1)} %copy.17.wgt), custom_call_target="tpu_custom_call" | custom-call | tf_op jit(solution)/shard_map/pallas_call | solution.py:349
  88.7 0.0 copy-done.2
  88.7 0.0 copy-start.3
  88.7 0.2 copy.18
  88.9 0.7 copy-done.3
  89.6 0.2 copy.20
  89.8 0.3 divide_subtract_fusion
  90.0 0.8 copy.22
  90.8 0.8 copy.23
  91.6 0.8 copy.24
  92.4 0.7 copy.27
  93.1 0.7 copy.28
Async XLA Ops:
  0.6 1.1 %copy-start = (bf16[1,4,32,640]{3,2,1,0:T(8,128)(2,1)S(1)}, bf16[1,4,32,640]{3,2,1,0:T(8,128)(2,1)}, u32[]{:S(2)}) copy-start(bf16[1,4,32,640]{3,2,1,0:T(8,128)(2,1)} %param.5) | copy-start | bytes 491524
  0.6 1.1 %copy-start.1 = (bf16[1,4,32,640]{3,2,1,0:T(8,128)(2,1)S(1)}, bf16[1,4,32,640]{3,2,1,0:T(8,128)(2,1)}, u32[]{:S(2)}) copy-start(bf16[1,4,32,640]{3,2,1,0:T(8,128)(2,1)} %param.6) | copy-start | bytes 491524
  1.8 86.9 %copy-start.2 = (f32[9,80,10]{1,2,0:T(8,128)S(1)}, f32[9,80,10]{1,2,0:T(8,128)}, u32[]{:S(2)}) copy-start(f32[9,80,10]{1,2,0:T(8,128)} %param.8) | copy-start | bytes 86404
  88.7 0.9 copy-start.3

commit v3 on v2

v3 whole, which is shorter than its diff:
```python
import jax
import jax.numpy as jnp
from jax import lax
from jax.experimental import pallas as pl
from jax.experimental.pallas import tpu as pltpu
from jax.sharding import PartitionSpec as P

MESH = pl.DeviceIdType.MESH
F32 = jnp.float32
BF16 = jnp.bfloat16
Y_ORDER = (1, 7, 2, 6, 3, 5, 4)
BLOCKS = (4, 3, 5, 2, 6, 1, 7, 0)
GROUPS = ((0, 384), (384, 640), (640, 1024))
N_SEM = 128
NT = (((1,), (1,)), ((), ()))
TN = (((0,), (0,)), ((), ()))


class Copy:
    def __init__(self, copy):
        self.copy, self.got, self.gone = copy, False, False
        copy.start()

    def recv(self):
        if not self.got:
            self.copy.wait_recv()
        self.got = True

    def sent(self):
        if not self.gone:
            self.copy.wait_send()
        self.gone = True


def dot(a, b, dims=(((1,), (0,)), ((), ()))):
    return lax.dot_general(a, b, dims, preferred_element_type=F32)


def kernel(
    lat, tgt, wgt, stu_out, ig_out, g_out,
    kp, km, xs, st, sk, ts, tb, tr, sb, rb, e3, gacc, gb, ga, ra, rs, rd, ysend, yr, zs, zr,
    igp, igr, igc, ia, isum, idr, send_sem, recv_sem,
):
    dp, row = lax.axis_index("dp"), lax.axis_index("rows")
    k, y, zh = dp % 2, (dp // 2) % 8, dp // 16
    x, zl = row % 4, row // 4

    def dev(dz=0, dy=0, flip=False, dx=0, flip_zl=False):
        core = 1 - k if flip else k
        low = 1 - zl if flip_zl else zl
        return (((zh + dz) % 4 * 8 + (y + dy) % 8) * 2 + core, low * 4 + (x + dx) % 4)

    def row_dev(dr):
        return (dp, (row + dr) % 8)

    copies = []

    def send(src, dst, device):
        i = len(copies)
        copy = pltpu.make_async_remote_copy(
            src_ref=src,
            dst_ref=dst,
            send_sem=send_sem.at[i],
            recv_sem=recv_sem.at[i],
            device_id=device,
            device_id_type=MESH,
        )
        copies.append(Copy(copy))
        return copies[i]

    def blk(dy):
        j = BLOCKS.index(dy % 8)
        return slice(j * 128, j * 128 + 128)

    def rows_of(dx, low):
        at = (zl if low == 0 else 1 - zl) * 4 + (x + dx) % 4
        return pl.ds(pl.multiple_of(at * 80, 16), 80)

    barrier = pltpu.get_barrier_semaphore()
    partners = [dev(flip_zl=True), dev(dx=1), dev(dx=-1), row_dev(1), row_dev(-1)]
    partners += [dev(dy=dy) for dy in Y_ORDER] + [dev(dz=dz) for dz in (1, 2, 3)]
    partners += [dev(dz=dz, flip=True) for dz in range(4)]
    for partner in partners:
        pl.semaphore_signal(barrier, inc=1, device_id=partner, device_id_type=MESH)

    fill = jnp.zeros((6, 80), F32)
    rows = jnp.concatenate([v for t in range(9) for v in (wgt[t], fill)], axis=0)
    l9 = lax.broadcasted_iota(jnp.int32, (144, 128), 1)
    n9 = lax.broadcasted_iota(jnp.int32, (144, 128), 0)
    pick = (n9 & 15 < 10) & (l9 == (n9 >> 4) * 10 + (n9 & 15))
    pick = jnp.where(pick, 1.0, 0.0).astype(BF16)
    kp[0, 0, :, blk(0)] = dot(rows.astype(BF16), pick, TN).astype(BF16)
    xs[0, 32:160] = lat[...]
    lane = lax.broadcasted_iota(jnp.int32, (640, 128), 1)
    chan = lax.broadcasted_iota(jnp.int32, (640, 128), 0)
    place = lane + 10 * ((lane * 205) >> 11)
    for s in range(8):
        core = k if s < 4 else 1 - k
        hit = (chan == place + (zh + s % 4) % 4 * 160 + core * 10) & (lane < 80)
        st[:, s * 128 : s * 128 + 128] = jnp.where(hit, 1.0, 0.0).astype(BF16)

    l0 = lax.broadcasted_iota(jnp.int32, (128, 768), 0)
    q = lax.broadcasted_iota(jnp.int32, (128, 768), 1)
    tap = (l0 * 205) >> 11
    third = (tap * 11) >> 5
    want = third * 256 + (tap - 3 * third) * 80 + l0 - 10 * tap
    diff = jnp.where(l0 < 90, q - want, -1)
    for j, dy in enumerate(BLOCKS):
        hit = jnp.where(diff == (y + dy) % 8 * 10, 1.0, 0.0)
        sk[j * 128 : j * 128 + 128, :] = hit.astype(BF16)

    pl.semaphore_wait(barrier, len(partners))
    p0 = send(kp.at[0, 0, :, blk(0)], kp.at[0, 1, :, blk(0)], dev(flip_zl=True))
    up0 = send(lat.at[0:64], xs.at[3, 32:96], dev(dz=1))
    dn1 = send(lat.at[64:128], xs.at[1, 96:160], dev(dz=-1))
    up1 = send(lat.at[64:128], xs.at[3, 96:160], dev(dz=1))
    dn0 = send(lat.at[0:64], xs.at[1, 32:96], dev(dz=-1))
    part = [send(lat, xs.at[4, 32:160], dev(flip=True))]
    top = [send(lat.at[0:32], xs.at[0, 160:192], row_dev(-1))]
    bot = [send(lat.at[96:128], xs.at[0, 0:32], row_dev(1))]

    p0.recv()
    block = kp.at[0, :, :, blk(0)]
    p1 = {dy: send(block, kp.at[0, :, :, blk(-dy)], dev(dy=dy)) for dy in Y_ORDER}
    right, left, fwd_r, fwd_l = {}, {}, {}, {}
    right[0] = send(block, kp.at[3, :, :, blk(0)], dev(dx=1))
    left[0] = send(block, kp.at[1, :, :, blk(0)], dev(dx=-1))

    def halos(s):
        top.append(send(xs.at[s, 32:64], xs.at[s, 160:192], row_dev(-1)))
        bot.append(send(xs.at[s, 128:160], xs.at[s, 0:32], row_dev(1)))

    up0.recv()
    over0 = send(xs.at[3, 32:96], xs.at[2, 32:96], dev(dz=1))
    dn1.recv()
    over1 = send(xs.at[1, 96:160], xs.at[2, 96:160], dev(dz=-1))

    def y_step(dy):
        p1[dy].recv()
        got = kp.at[0, :, :, blk(-dy)]
        right[dy] = send(got, kp.at[3, :, :, blk(-dy)], dev(dx=1))
        left[dy] = send(got, kp.at[1, :, :, blk(-dy)], dev(dx=-1))

    def x_step(dy):
        right[dy].recv()
        dst = kp.at[2, 0, :, blk(-dy)]
        fwd_r[dy] = send(kp.at[3, 0, :, blk(-dy)], dst, dev(dx=1))
        left[dy].recv()
        dst = kp.at[2, 1, :, blk(-dy)]
        fwd_l[dy] = send(kp.at[1, 1, :, blk(-dy)], dst, dev(dx=-1))

    y_step(1)
    y_step(7)
    x_step(0)
    up1.recv()
    halos(3)
    part.append(send(xs.at[3, 32:160], xs.at[7, 32:160], dev(flip=True)))
    dn0.recv()
    halos(1)
    part.append(send(xs.at[1, 32:160], xs.at[5, 32:160], dev(flip=True)))
    y_step(2)
    y_step(6)
    x_step(1)
    x_step(7)

    ts[...] = dot(st[...], tgt[...], (((0,), (1,)), ((), ()))).astype(BF16)
    tsent = []
    for s in (4, 1, 3, 5, 7):
        back = s // 4 * 4 + (-s) % 4
        src = ts.at[s * 128 : s * 128 + 80]
        tsent.append(send(src, tb.at[back], dev(dz=s % 4, flip=s >= 4)))
    two_up = send(ts.at[256:336], tr.at[0], dev(dz=1))
    two_dn = send(ts.at[768:848], tr.at[1], dev(dz=-1))
    tb[0] = ts[0:80]

    y_step(3)
    y_step(5)
    y_step(4)
    x_step(2)
    x_step(6)
    over0.recv()
    over1.recv()
    halos(2)
    part.append(send(xs.at[2, 32:160], xs.at[6, 32:160], dev(flip=True)))
    two_up.recv()
    tsent.append(send(tr.at[0], tb.at[2], dev(dz=1)))
    two_dn.recv()
    tsent.append(send(tr.at[1], tb.at[6], dev(dz=-1, flip=True)))
    x_step(3)
    x_step(5)
    x_step(4)

    def place_kernel(dx):
        out = dot(kp[dx].reshape(160, 1024), sk[...]).astype(BF16)
        km[rows_of(dx, 0), :] = out[:80]
        km[rows_of(dx, 1), :] = out[80:]

    place_kernel(0)
    place_kernel(1)
    place_kernel(3)

    for c in top + bot:
        c.recv()
    part.append(send(xs.at[0:4, 0:32], xs.at[4:8, 0:32], dev(flip=True)))
    part.append(send(xs.at[0:4, 160:192], xs.at[4:8, 160:192], dev(flip=True)))
    for dy in (0,) + Y_ORDER:
        fwd_r[dy].recv()
        fwd_l[dy].recv()
    place_kernel(2)
    for c in part:
        c.recv()
    part[-1].sent()
    part[-2].sent()

    @pl.when(row == 0)
    def _():
        xs[:, 0:32, :] = jnp.zeros((8, 32, 640), BF16)

    @pl.when(row == 7)
    def _():
        xs[:, 160:192, :] = jnp.zeros((8, 32, 640), BF16)

    for c in tsent:
        c.recv()

    col = lax.broadcasted_iota(jnp.int32, (256, 128), 0) % 32
    first, last = col == 0, col == 31
    real = lax.broadcasted_iota(jnp.int32, (256, 128), 1) < 80

    def forward(m, carry):
        two = pl.ds(2 * m, 2)
        acc = None
        for a in range(3):
            win = xs[two, 32 * a : 32 * a + 128, :].reshape(256, 640)
            term = dot(win, km[:, 256 * a : 256 * a + 256])
            acc = term if acc is None else acc + term
        mid = pltpu.roll(acc, 176, 1)[:, :128]
        end = pltpu.roll(acc, 96, 1)[:, :128]
        total = mid + jnp.where(first, 0.0, pltpu.roll(acc[:, :128], 1, 0))
        total = total + jnp.where(last, 0.0, pltpu.roll(end, 255, 0))
        stu = jnp.where(real, total, 0.0).astype(BF16)
        sb[two] = stu.reshape(2, 128, 128)
        pair, fill = tb[two].astype(F32), jnp.zeros((48, 128), F32)
        goal = [jnp.concatenate([pair[i], fill], axis=0).T for i in range(2)]
        err = stu.astype(F32) - jnp.concatenate(goal, axis=0)
        err = err.astype(BF16).astype(F32)
        zero = jnp.zeros((256, 128), F32)
        nxt = jnp.where(last, 0.0, pltpu.roll(err, 255, 0))
        prv = jnp.where(first, 0.0, pltpu.roll(err, 1, 0))
        wide = jnp.concatenate([nxt, zero], axis=1)
        wide = wide + pltpu.roll(jnp.concatenate([err, zero], axis=1), 80, 1)
        wide = wide + pltpu.roll(jnp.concatenate([prv, zero], axis=1), 160, 1)
        e3[two, 32:160, :] = wide.astype(BF16).reshape(2, 128, 256)
        return carry

    lax.fori_loop(0, 4, forward, 0)

    etop = send(e3.at[:, 32:64], e3.at[:, 160:192], row_dev(-1))
    ebot = send(e3.at[:, 128:160], e3.at[:, 0:32], row_dev(1))
    ssent = []
    for s in (4, 1, 3, 5, 7, 2, 6):
        back = s // 4 * 4 + (-s) % 4
        dst = rb.at[:, back * 128 : back * 128 + 128]
        ssent.append(send(sb.at[s], dst, dev(dz=s % 4, flip=s >= 4)))
    rb[:, 0:128] = sb[0]

    gacc[...] = jnp.zeros((640, 768), F32)

    def weight_grad(m, carry):
        two = pl.ds(2 * m, 2)
        errs = e3[two, 32:160, :].reshape(256, 256)
        for a in range(3):
            win = xs[two, 32 * a : 32 * a + 128, :].reshape(256, 640)
            gacc[:, 256 * a : 256 * a + 256] += dot(win, errs, TN)
        return carry

    lax.fori_loop(0, 4, weight_grad, 0)
    gb[...] = gacc[...].astype(BF16)

    first_hop, raw, second_hop = [], [], []
    for lo, hi in GROUPS:
        cols = slice(lo, hi)
        ga[:, cols] = dot(gb[...], sk[cols, :], NT).astype(BF16)
        up = send(ga.at[rows_of(2, 0), cols], ra.at[0, :, cols], dev(dx=1))
        dn = send(ga.at[rows_of(2, 1), cols], ra.at[1, :, cols], dev(dx=-1))
        first_hop.append((up, dn))
        up = send(ga.at[rows_of(1, 1), cols], rd.at[1, :, cols], dev(dx=1))
        dn = send(ga.at[rows_of(3, 0), cols], rd.at[0, :, cols], dev(dx=-1))
        raw.append((up, dn))

    def relay(g):
        cols = slice(*GROUPS[g])
        up, dn = first_hop[g]
        up.recv()
        rs[0, :, cols] = (ra[0, :, cols].astype(F32) + ga[rows_of(1, 0), cols].astype(F32)).astype(BF16)
        up = send(rs.at[0, :, cols], rd.at[2, :, cols], dev(dx=1))
        dn.recv()
        rs[1, :, cols] = (ra[1, :, cols].astype(F32) + ga[rows_of(3, 1), cols].astype(F32)).astype(BF16)
        dn = send(rs.at[1, :, cols], rd.at[3, :, cols], dev(dx=-1))
        second_hop.append((up, dn))

    ysent = []

    def spread(g):
        cols = slice(*GROUPS[g])
        for c in raw[g] + second_hop[g]:
            c.recv()
        for i in range(2):
            mine = ga[rows_of(0, i), cols].astype(F32)
            both = rd[i, :, cols].astype(F32) + rd[i + 2, :, cols].astype(F32)
            ysend[i, :, cols] = (mine + both).astype(BF16)
        for dy in BLOCKS[GROUPS[g][0] // 128 : GROUPS[g][1] // 128]:
            if dy:
                ysent.append(send(ysend.at[:, :, blk(dy)], yr.at[len(ysent)], dev(dy=dy)))

    etop.recv()
    ebot.recv()
    etop.sent()
    ebot.sent()

    @pl.when(row == 0)
    def _():
        e3[:, 0:32, :] = jnp.zeros((8, 32, 256), BF16)

    @pl.when(row == 7)
    def _():
        e3[:, 160:192, :] = jnp.zeros((8, 32, 256), BF16)

    def input_grad(m, carry):
        two = pl.ds(2 * m, 2)
        acc = None
        for a in range(3):
            win = e3[two, 64 - 32 * a : 192 - 32 * a, :].reshape(256, 256)
            term = dot(win, km[:, 256 * a : 256 * a + 256], NT)
            acc = term if acc is None else acc + term
        igp[two] = acc.astype(BF16).reshape(2, 128, 640)
        return carry

    lax.fori_loop(2, 3, input_grad, 0)
    relay(0)
    lax.fori_loop(3, 4, input_grad, 0)
    ip = send(igp.at[4:8], igr, dev(flip=True))
    relay(1)
    lax.fori_loop(0, 1, input_grad, 0)
    relay(2)
    spread(0)
    lax.fori_loop(1, 2, input_grad, 0)
    spread(1)
    ip.recv()
    for s in (2, 1, 3, 0):
        igc[s] = (igp[s].astype(F32) + igr[s].astype(F32)).astype(BF16)
        if s == 2:
            ir_a = send(igc.at[2, 0:64], ia.at[0], dev(dz=1))
            ir_b = send(igc.at[2, 64:128], ia.at[1], dev(dz=-1))
        if s == 1:
            id_a = send(igc.at[1, 64:128], idr.at[1], dev(dz=1))
        if s == 3:
            id_b = send(igc.at[3, 0:64], idr.at[0], dev(dz=-1))
    spread(2)

    ir_a.recv()
    isum[0] = (ia[0].astype(F32) + igc[1, 0:64].astype(F32)).astype(BF16)
    is_a = send(isum.at[0], idr.at[2], dev(dz=1))
    ir_b.recv()
    isum[1] = (ia[1].astype(F32) + igc[3, 64:128].astype(F32)).astype(BF16)
    is_b = send(isum.at[1], idr.at[3], dev(dz=-1))

    for c in ssent:
        c.recv()
    stu_out[...] = dot(rb[...], st[...], NT).astype(BF16)

    total = ysend[:, :, blk(0)].astype(F32)
    for i in range(7):
        ysent[i].recv()
        total = total + yr[i].astype(F32)
    zs[...] = total
    zc = send(zs.at[1], zr, dev(flip_zl=True))

    for c in (id_a, id_b, is_a, is_b):
        c.recv()
    low = igc[0, 0:64].astype(F32) + idr[0].astype(F32) + idr[2].astype(F32)
    high = igc[0, 64:128].astype(F32) + idr[1].astype(F32) + idr[3].astype(F32)
    ig_out[0:64] = low.astype(BF16)
    ig_out[64:128] = high.astype(BF16)

    zc.recv()
    grad = (zs[0] + zr[...]) * (1.0 / 64.0)
    turned = jnp.concatenate([grad, jnp.zeros((48, 128), F32)], axis=0).T
    for t in range(9):
        g_out[t] = turned[10 * t : 10 * t + 10, :80]
    for c in copies:
        c.sent()


def per_device(latents, target, weight, moment1, moment2):
    vmem = pl.BlockSpec(memory_space=pltpu.VMEM)
    student, input_grad, grad = pl.pallas_call(
        kernel,
        out_shape=(
            jax.ShapeDtypeStruct((128, 640), BF16),
            jax.ShapeDtypeStruct((128, 640), BF16),
            jax.ShapeDtypeStruct((9, 10, 80), F32),
        ),
        in_specs=[vmem] * 3,
        out_specs=(vmem,) * 3,
        scratch_shapes=[
            pltpu.VMEM((4, 2, 80, 1024), BF16),
            pltpu.VMEM((640, 768), BF16),
            pltpu.VMEM((8, 192, 640), BF16),
            pltpu.VMEM((640, 1024), BF16),
            pltpu.VMEM((1024, 768), BF16),
            pltpu.VMEM((1024, 128), BF16),
            pltpu.VMEM((8, 80, 128), BF16),
            pltpu.VMEM((2, 80, 128), BF16),
            pltpu.VMEM((8, 128, 128), BF16),
            pltpu.VMEM((128, 1024), BF16),
            pltpu.VMEM((8, 192, 256), BF16),
            pltpu.VMEM((640, 768), F32),
            pltpu.VMEM((640, 768), BF16),
            pltpu.VMEM((640, 1024), BF16),
            pltpu.VMEM((2, 80, 1024), BF16),
            pltpu.VMEM((2, 80, 1024), BF16),
            pltpu.VMEM((4, 80, 1024), BF16),
            pltpu.VMEM((2, 80, 1024), BF16),
            pltpu.VMEM((7, 2, 80, 128), BF16),
            pltpu.VMEM((2, 80, 128), F32),
            pltpu.VMEM((80, 128), F32),
            pltpu.VMEM((8, 128, 640), BF16),
            pltpu.VMEM((4, 128, 640), BF16),
            pltpu.VMEM((4, 128, 640), BF16),
            pltpu.VMEM((2, 64, 640), BF16),
            pltpu.VMEM((2, 64, 640), BF16),
            pltpu.VMEM((4, 64, 640), BF16),
            pltpu.SemaphoreType.DMA((N_SEM,)),
            pltpu.SemaphoreType.DMA((N_SEM,)),
        ],
        compiler_params=pltpu.CompilerParams(
            collective_id=0, has_side_effects=True, vmem_limit_bytes=48 << 20
        ),
    )(latents.reshape(128, 640), target.reshape(128, 640), weight.transpose(0, 2, 1))
    grad = grad.transpose(0, 2, 1)
    new_moment1 = 0.9 * moment1 + 0.1 * grad
    new_moment2 = 0.999 * moment2 + 0.001 * grad * grad
    new_weight = weight - 0.01 * new_moment1 / (jnp.sqrt(new_moment2) + 1e-08)
    return (
        student.reshape(latents.shape),
        input_grad.reshape(latents.shape),
        new_weight,
        new_moment1,
        new_moment2,
    )


def solution(mesh):
    act = P("dp", "rows", None, None)
    par = P(None, "rows", "dp")
    return jax.shard_map(
        per_device,
        mesh=mesh,
        in_specs=(act, act, par, par, par),
        out_specs=(act, act, par, par, par),
        check_vma=False,
    )
```

time: 94.8 us -> 78.9 us (0.83)
  the two profiles are of different devices: /device:TPU:1 before, /device:TPU:6 now
where the time goes in v3:
time: 78.9 us; the launch traced here: 78.7 us
  Pallas kernels  73.3 us (93%)
  local copies, waits for them, and re-layouts  4.05 us (5%)
    pallas_call x1, Pallas kernels, per_device(): pl.pallas_call(kernel, out_shape=(jax.ShapeDtypeStruct((128, 640), BF16),...  73.3 us
    unnamed x12, local copies, waits for them, and re-layouts  4.05 us

profile of v3, /device:TPU:6, one launch (start us, length us, event | category | flops | bytes accessed | tf_op | source)
XLA Modules:
  0.0 78.7 jit_solution(1238313161386144451)
XLA Ops:
  0.6 0.0 copy-start
  0.6 0.9 %copy-done = f32[9,80,10]{1,2,0:T(8,128)S(1)} copy-done((f32[9,80,10]{1,2,0:T(8,128)S(1)}, f32[9,80,10]{1,2,0:T(8,128)}, u32[]{:S(2)}) %copy-start) | copy-done | bytes 28824
  1.5 0.0 copy-start.1
  1.5 0.9 %copy-done.1 = bf16[1,4,32,640]{3,2,1,0:T(8,128)(2,1)S(1)} copy-done((bf16[1,4,32,640]{3,2,1,0:T(8,128)(2,1)S(1)}, bf16[1,4,32,640]{3,2,1,0:T(8,128)(2,1)}, u32[]{:S(2)}) %copy-start.1) | copy-done | bytes 163864
  2.4 0.0 copy-start.2
  2.4 0.9 %copy-done.2 = bf16[1,4,32,640]{3,2,1,0:T(8,128)(2,1)S(1)} copy-done((bf16[1,4,32,640]{3,2,1,0:T(8,128)(2,1)S(1)}, bf16[1,4,32,640]{3,2,1,0:T(8,128)(2,1)}, u32[]{:S(2)}) %copy-start.2) | copy-done | bytes 163864
  3.4 0.0 copy-start.3
  3.4 0.0 copy-start.4
  3.4 73.3 %shard_map.92 = (bf16[128,640]{1,0:T(8,128)(2,1)S(1)}, bf16[128,640]{1,0:T(8,128)(2,1)S(1)}, f32[9,10,80]{2,1,0:T(8,128)S(1)}) custom-call(bf16[128,640]{1,0:T(8,128)(2,1)S(1)} %bitcast.13, bf16[128,640]{1,0:T(8,128)(2,1)S(1)} %bitcast.14, f32[9,10,80]{2,1,0:T(8,128)S(1)} %bitcast.12), custom_call_target="tpu_custom_call" | custom-call | tf_op jit(solution)/shard_map/pallas_call | solution.py:397
  76.7 0.0 copy-done.3
  76.7 0.0 copy-done.4
  76.7 0.7 divide_subtract_fusion
  77.4 0.7 copy.12
  78.0 0.7 copy.13
Async XLA Ops:
  0.6 0.9 %copy-start = (f32[9,80,10]{1,2,0:T(8,128)S(1)}, f32[9,80,10]{1,2,0:T(8,128)}, u32[]{:S(2)}) copy-start(f32[9,80,10]{1,2,0:T(8,128)} %param.7) | copy-start | bytes 86404
  1.5 0.9 %copy-start.1 = (bf16[1,4,32,640]{3,2,1,0:T(8,128)(2,1)S(1)}, bf16[1,4,32,640]{3,2,1,0:T(8,128)(2,1)}, u32[]{:S(2)}) copy-start(bf16[1,4,32,640]{3,2,1,0:T(8,128)(2,1)} %param.5) | copy-start | bytes 491524
  2.4 0.9 %copy-start.2 = (bf16[1,4,32,640]{3,2,1,0:T(8,128)(2,1)S(1)}, bf16[1,4,32,640]{3,2,1,0:T(8,128)(2,1)}, u32[]{:S(2)}) copy-start(bf16[1,4,32,640]{3,2,1,0:T(8,128)(2,1)} %param.6) | copy-start | bytes 491524
  3.4 73.3 %copy-start.3 = (f32[9,80,10]{1,2,0:T(8,128)S(1)}, f32[9,80,10]{1,2,0:T(8,128)}, u32[]{:S(2)}) copy-start(f32[9,80,10]{1,2,0:T(8,128)} %param.8) | copy-start | bytes 86404
  3.4 73.3 %copy-start.4 = (f32[9,80,10]{1,2,0:T(8,128)S(1)}, f32[9,80,10]{1,2,0:T(8,128)}, u32[]{:S(2)}) copy-start(f32[9,80,10]{1,2,0:T(8,128)} %param.9) | copy-start | bytes 86404

commit v4 on v3

--- a/solution.py
+++ b/solution.py
@@ -11,7 +11,7 @@
 Y_ORDER = (1, 7, 2, 6, 3, 5, 4)
 BLOCKS = (4, 3, 5, 2, 6, 1, 7, 0)
 GROUPS = ((0, 384), (384, 640), (640, 1024))
-N_SEM = 128
+N_SEM = 160
 NT = (((1,), (1,)), ((), ()))
 TN = (((0,), (0,)), ((), ()))
 
@@ -37,9 +37,9 @@
 
 
 def kernel(
-    lat, tgt, wgt, stu_out, ig_out, g_out,
-    kp, km, xs, st, sk, ts, tb, tr, sb, rb, e3, gacc, gb, ga, ra, rs, rd, ysend, yr, zs, zr,
-    igp, igr, igc, ia, isum, idr, send_sem, recv_sem,
+    lat_in, tgt_in, wgt_in, stu_out, ig_out, g_out,
+    kp, km, xs, st, sk, ts, tb, tr, sb, sr, rb, e3, gacc, gb, ga, ra, rs, rd, ysend, yr, zs, zr,
+    igp, igr, igc, ia, isum, idr, tgt, wgt, load_sem, send_sem, recv_sem,
 ):
     dp, row = lax.axis_index("dp"), lax.axis_index("rows")
     k, y, zh = dp % 2, (dp // 2) % 8, dp // 16
@@ -76,6 +76,12 @@
         at = (zl if low == 0 else 1 - zl) * 4 + (x + dx) % 4
         return pl.ds(pl.multiple_of(at * 80, 16), 80)
 
+    lat = xs.at[0, 32:160]
+    loads = []
+    for i, (src, dst) in enumerate(((wgt_in, wgt), (lat_in, lat), (tgt_in, tgt))):
+        loads.append(pltpu.make_async_copy(src, dst, load_sem.at[i]))
+        loads[i].start()
+
     barrier = pltpu.get_barrier_semaphore()
     partners = [dev(flip_zl=True), dev(dx=1), dev(dx=-1), row_dev(1), row_dev(-1)]
     partners += [dev(dy=dy) for dy in Y_ORDER] + [dev(dz=dz) for dz in (1, 2, 3)]
@@ -83,14 +89,6 @@
     for partner in partners:
         pl.semaphore_signal(barrier, inc=1, device_id=partner, device_id_type=MESH)
 
-    fill = jnp.zeros((6, 80), F32)
-    rows = jnp.concatenate([v for t in range(9) for v in (wgt[t], fill)], axis=0)
-    l9 = lax.broadcasted_iota(jnp.int32, (144, 128), 1)
-    n9 = lax.broadcasted_iota(jnp.int32, (144, 128), 0)
-    pick = (n9 & 15 < 10) & (l9 == (n9 >> 4) * 10 + (n9 & 15))
-    pick = jnp.where(pick, 1.0, 0.0).astype(BF16)
-    kp[0, 0, :, blk(0)] = dot(rows.astype(BF16), pick, TN).astype(BF16)
-    xs[0, 32:160] = lat[...]
     lane = lax.broadcasted_iota(jnp.int32, (640, 128), 1)
     chan = lax.broadcasted_iota(jnp.int32, (640, 128), 0)
     place = lane + 10 * ((lane * 205) >> 11)
@@ -109,37 +107,60 @@
         hit = jnp.where(diff == (y + dy) % 8 * 10, 1.0, 0.0)
         sk[j * 128 : j * 128 + 128, :] = hit.astype(BF16)
 
+    loads[0].wait()
+    fill = jnp.zeros((6, 80), F32)
+    rows = jnp.concatenate([v for t in range(9) for v in (wgt[t], fill)], axis=0)
+    l9 = lax.broadcasted_iota(jnp.int32, (144, 128), 1)
+    n9 = lax.broadcasted_iota(jnp.int32, (144, 128), 0)
+    pick = (n9 & 15 < 10) & (l9 == (n9 >> 4) * 10 + (n9 & 15))
+    pick = jnp.where(pick, 1.0, 0.0).astype(BF16)
+    kp[0, 0, :, blk(0)] = dot(rows.astype(BF16), pick, TN).astype(BF16)
+    rb[...] = jnp.zeros((1024, 128), BF16)
+    loads[2].wait()
+    ts[...] = dot(st[...], tgt[...], (((0,), (1,)), ((), ()))).astype(BF16)
+    tb[0] = ts[0:80]
+    loads[1].wait()
     pl.semaphore_wait(barrier, len(partners))
     p0 = send(kp.at[0, 0, :, blk(0)], kp.at[0, 1, :, blk(0)], dev(flip_zl=True))
     up0 = send(lat.at[0:64], xs.at[3, 32:96], dev(dz=1))
     dn1 = send(lat.at[64:128], xs.at[1, 96:160], dev(dz=-1))
     up1 = send(lat.at[64:128], xs.at[3, 96:160], dev(dz=1))
     dn0 = send(lat.at[0:64], xs.at[1, 32:96], dev(dz=-1))
-    part = [send(lat, xs.at[4, 32:160], dev(flip=True))]
+    part = {0: send(lat, xs.at[4, 32:160], dev(flip=True))}
     top = [send(lat.at[0:32], xs.at[0, 160:192], row_dev(-1))]
     bot = [send(lat.at[96:128], xs.at[0, 0:32], row_dev(1))]
 
     p0.recv()
     block = kp.at[0, :, :, blk(0)]
-    p1 = {dy: send(block, kp.at[0, :, :, blk(-dy)], dev(dy=dy)) for dy in Y_ORDER}
+    p1, late = {}, {}
+    for dy in (2, -2, 1, -1):
+        p1[dy] = send(block, kp.at[0, :, :, blk(-dy)], dev(dy=dy))
     right, left, fwd_r, fwd_l = {}, {}, {}, {}
     right[0] = send(block, kp.at[3, :, :, blk(0)], dev(dx=1))
     left[0] = send(block, kp.at[1, :, :, blk(0)], dev(dx=-1))
 
+    halo = {0: (top[0], bot[0])}
+
     def halos(s):
-        top.append(send(xs.at[s, 32:64], xs.at[s, 160:192], row_dev(-1)))
-        bot.append(send(xs.at[s, 128:160], xs.at[s, 0:32], row_dev(1)))
-
-    up0.recv()
-    over0 = send(xs.at[3, 32:96], xs.at[2, 32:96], dev(dz=1))
-    dn1.recv()
-    over1 = send(xs.at[1, 96:160], xs.at[2, 96:160], dev(dz=-1))
-
-    def y_step(dy):
-        p1[dy].recv()
+        up = send(xs.at[s, 32:64], xs.at[s, 160:192], row_dev(-1))
+        dn = send(xs.at[s, 128:160], xs.at[s, 0:32], row_dev(1))
+        halo[s] = (up, dn)
+        part[s] = send(xs.at[s, 32:160], xs.at[s + 4, 32:160], dev(flip=True))
+
+    def x_sends(dy):
         got = kp.at[0, :, :, blk(-dy)]
         right[dy] = send(got, kp.at[3, :, :, blk(-dy)], dev(dx=1))
         left[dy] = send(got, kp.at[1, :, :, blk(-dy)], dev(dx=-1))
+
+    def y_near(dy):
+        p1[dy].recv()
+        if dy in (2, -2):
+            one, half = dy // 2, 0 if dy > 0 else 1
+            got = kp.at[0, :, :, blk(-dy)]
+            p1[dy + one] = send(got, kp.at[0, :, :, blk(-dy - one)], dev(dy=one))
+            dst = kp.at[0, half, :, blk(4)]
+            late[half] = send(kp.at[0, half, :, blk(-dy)], dst, dev(dy=dy))
+        x_sends(dy)
 
     def x_step(dy):
         right[dy].recv()
@@ -149,45 +170,51 @@
         dst = kp.at[2, 1, :, blk(-dy)]
         fwd_l[dy] = send(kp.at[1, 1, :, blk(-dy)], dst, dev(dx=-1))
 
-    y_step(1)
-    y_step(7)
+    def to_group(src_of, dst_of, hops):
+        sent = {}
+        for s in (4, 1, 3, 5, 7):
+            back = s // 4 * 4 + (-s) % 4
+            sent[back] = send(src_of(s), dst_of(back), dev(dz=s % 4, flip=s >= 4))
+        up = send(src_of(2), hops.at[0], dev(dz=1))
+        dn = send(src_of(6), hops.at[1], dev(dz=-1))
+
+        def relay_up():
+            up.recv()
+            sent[2] = send(hops.at[0], dst_of(2), dev(dz=1))
+
+        def relay_dn():
+            dn.recv()
+            sent[6] = send(hops.at[1], dst_of(6), dev(dz=-1, flip=True))
+
+        return sent, relay_up, relay_dn
+
+    y_near(2)
+    y_near(-2)
+    y_near(1)
+    y_near(-1)
     x_step(0)
+    up0.recv()
+    over0 = send(xs.at[3, 32:96], xs.at[2, 32:96], dev(dz=1))
+    dn1.recv()
+    over1 = send(xs.at[1, 96:160], xs.at[2, 96:160], dev(dz=-1))
+    goals, goal_up, goal_dn = to_group(
+        lambda s: ts.at[s * 128 : s * 128 + 80], lambda s: tb.at[s], tr
+    )
+    x_step(2)
+    x_step(-2)
+    y_near(3)
+    y_near(-3)
+    late[0].recv()
+    late[1].recv()
+    x_sends(4)
+    x_step(1)
+    x_step(-1)
     up1.recv()
     halos(3)
-    part.append(send(xs.at[3, 32:160], xs.at[7, 32:160], dev(flip=True)))
     dn0.recv()
     halos(1)
-    part.append(send(xs.at[1, 32:160], xs.at[5, 32:160], dev(flip=True)))
-    y_step(2)
-    y_step(6)
-    x_step(1)
-    x_step(7)
-
-    ts[...] = dot(st[...], tgt[...], (((0,), (1,)), ((), ()))).astype(BF16)
-    tsent = []
-    for s in (4, 1, 3, 5, 7):
-        back = s // 4 * 4 + (-s) % 4
-        src = ts.at[s * 128 : s * 128 + 80]
-        tsent.append(send(src, tb.at[back], dev(dz=s % 4, flip=s >= 4)))
-    two_up = send(ts.at[256:336], tr.at[0], dev(dz=1))
-    two_dn = send(ts.at[768:848], tr.at[1], dev(dz=-1))
-    tb[0] = ts[0:80]
-
-    y_step(3)
-    y_step(5)
-    y_step(4)
-    x_step(2)
-    x_step(6)
-    over0.recv()
-    over1.recv()
-    halos(2)
-    part.append(send(xs.at[2, 32:160], xs.at[6, 32:160], dev(flip=True)))
-    two_up.recv()
-    tsent.append(send(tr.at[0], tb.at[2], dev(dz=1)))
-    two_dn.recv()
-    tsent.append(send(tr.at[1], tb.at[6], dev(dz=-1, flip=True)))
     x_step(3)
-    x_step(5)
+    x_step(-3)
     x_step(4)
 
     def place_kernel(dx):
@@ -199,39 +226,52 @@
     place_kernel(1)
     place_kernel(3)
 
-    for c in top + bot:
-        c.recv()
-    part.append(send(xs.at[0:4, 0:32], xs.at[4:8, 0:32], dev(flip=True)))
-    part.append(send(xs.at[0:4, 160:192], xs.at[4:8, 160:192], dev(flip=True)))
-    for dy in (0,) + Y_ORDER:
+    over0.recv()
+    over1.recv()
+    halos(2)
+    goal_up()
+    goal_dn()
+    for dy in range(8):
+        dy = dy if dy < 5 else dy - 8
         fwd_r[dy].recv()
         fwd_l[dy].recv()
     place_kernel(2)
-    for c in part:
-        c.recv()
-    part[-1].sent()
-    part[-2].sent()
-
-    @pl.when(row == 0)
-    def _():
-        xs[:, 0:32, :] = jnp.zeros((8, 32, 640), BF16)
-
-    @pl.when(row == 7)
-    def _():
-        xs[:, 160:192, :] = jnp.zeros((8, 32, 640), BF16)
-
-    for c in tsent:
-        c.recv()
 
     col = lax.broadcasted_iota(jnp.int32, (256, 128), 0) % 32
     first, last = col == 0, col == 31
     real = lax.broadcasted_iota(jnp.int32, (256, 128), 1) < 80
 
-    def forward(m, carry):
-        two = pl.ds(2 * m, 2)
+    def pair_ready(s):
+        ends = []
+        for c, edge in zip(halo[s], (slice(160, 192), slice(0, 32))):
+            c.recv()
+            ends.append(send(xs.at[s, edge], xs.at[s + 4, edge], dev(flip=True)))
+        part[s].recv()
+        for c in ends:
+            c.recv()
+            c.sent()
+
+        @pl.when(row == 0)
+        def _():
+            xs[s, 0:32, :] = jnp.zeros((32, 640), BF16)
+            xs[s + 4, 0:32, :] = jnp.zeros((32, 640), BF16)
+
+        @pl.when(row == 7)
+        def _():
+            xs[s, 160:192, :] = jnp.zeros((32, 640), BF16)
+            xs[s + 4, 160:192, :] = jnp.zeros((32, 640), BF16)
+
+        for back in (s, s + 4):
+            if back:
+                goals[back].recv()
+
+    def joined(ref, s, rows):
+        return jnp.concatenate([ref[s, rows], ref[s + 4, rows]], axis=0)
+
+    def forward(s):
         acc = None
         for a in range(3):
-            win = xs[two, 32 * a : 32 * a + 128, :].reshape(256, 640)
+            win = joined(xs, s, slice(32 * a, 32 * a + 128))
             term = dot(win, km[:, 256 * a : 256 * a + 256])
             acc = term if acc is None else acc + term
         mid = pltpu.roll(acc, 176, 1)[:, :128]
@@ -239,10 +279,13 @@
         total = mid + jnp.where(first, 0.0, pltpu.roll(acc[:, :128], 1, 0))
         total = total + jnp.where(last, 0.0, pltpu.roll(end, 255, 0))
         stu = jnp.where(real, total, 0.0).astype(BF16)
-        sb[two] = stu.reshape(2, 128, 128)
-        pair, fill = tb[two].astype(F32), jnp.zeros((48, 128), F32)
-        goal = [jnp.concatenate([pair[i], fill], axis=0).T for i in range(2)]
-        err = stu.astype(F32) - jnp.concatenate(goal, axis=0)
+        stu = stu.astype(F32)
+        goal = []
+        for i, at in enumerate((s, s + 4)):
+            sb[at] = stu[128 * i : 128 * i + 128].T[:80].astype(BF16)
+            fill = jnp.zeros((48, 128), F32)
+            goal.append(jnp.concatenate([tb[at].astype(F32), fill], axis=0).T)
+        err = stu - jnp.concatenate(goal, axis=0)
         err = err.astype(BF16).astype(F32)
         zero = jnp.zeros((256, 128), F32)
         nxt = jnp.where(last, 0.0, pltpu.roll(err, 255, 0))
@@ -250,19 +293,20 @@
         wide = jnp.concatenate([nxt, zero], axis=1)
         wide = wide + pltpu.roll(jnp.concatenate([err, zero], axis=1), 80, 1)
         wide = wide + pltpu.roll(jnp.concatenate([prv, zero], axis=1), 160, 1)
-        e3[two, 32:160, :] = wide.astype(BF16).reshape(2, 128, 256)
-        return carry
-
-    lax.fori_loop(0, 4, forward, 0)
+        wide = wide.astype(BF16)
+        e3[s, 32:160, :] = wide[:128]
+        e3[s + 4, 32:160, :] = wide[128:]
+
+    for s in (0, 3, 1, 2):
+        pair_ready(s)
+        forward(s)
 
     etop = send(e3.at[:, 32:64], e3.at[:, 160:192], row_dev(-1))
     ebot = send(e3.at[:, 128:160], e3.at[:, 0:32], row_dev(1))
-    ssent = []
-    for s in (4, 1, 3, 5, 7, 2, 6):
-        back = s // 4 * 4 + (-s) % 4
-        dst = rb.at[:, back * 128 : back * 128 + 128]
-        ssent.append(send(sb.at[s], dst, dev(dz=s % 4, flip=s >= 4)))
-    rb[:, 0:128] = sb[0]
+    stus, stu_up, stu_dn = to_group(
+        lambda s: sb.at[s], lambda s: rb.at[s * 128 : s * 128 + 80], sr
+    )
+    rb[0:80] = sb[0]
 
     gacc[...] = jnp.zeros((640, 768), F32)
 
@@ -278,8 +322,9 @@
     gb[...] = gacc[...].astype(BF16)
 
     first_hop, raw, second_hop = [], [], []
-    for lo, hi in GROUPS:
-        cols = slice(lo, hi)
+
+    def place_grad(g):
+        cols = slice(*GROUPS[g])
         ga[:, cols] = dot(gb[...], sk[cols, :], NT).astype(BF16)
         up = send(ga.at[rows_of(2, 0), cols], ra.at[0, :, cols], dev(dx=1))
         dn = send(ga.at[rows_of(2, 1), cols], ra.at[1, :, cols], dev(dx=-1))
@@ -313,6 +358,7 @@
             if dy:
                 ysent.append(send(ysend.at[:, :, blk(dy)], yr.at[len(ysent)], dev(dy=dy)))
 
+    place_grad(0)
     etop.recv()
     ebot.recv()
     etop.sent()
@@ -326,37 +372,43 @@
     def _():
         e3[:, 160:192, :] = jnp.zeros((8, 32, 256), BF16)
 
-    def input_grad(m, carry):
-        two = pl.ds(2 * m, 2)
+    ip = {}
+
+    def input_grad(s):
         acc = None
         for a in range(3):
-            win = e3[two, 64 - 32 * a : 192 - 32 * a, :].reshape(256, 256)
+            win = e3[s : s + 2, 64 - 32 * a : 192 - 32 * a, :].reshape(256, 256)
             term = dot(win, km[:, 256 * a : 256 * a + 256], NT)
             acc = term if acc is None else acc + term
-        igp[two] = acc.astype(BF16).reshape(2, 128, 640)
-        return carry
-
-    lax.fori_loop(2, 3, input_grad, 0)
+        igp[s : s + 2] = acc.astype(BF16).reshape(2, 128, 640)
+        if s >= 4:
+            ip[s - 4] = send(igp.at[s : s + 2], igr.at[s - 4 : s - 2], dev(flip=True))
+
+    def core_sum(s):
+        igc[s] = (igp[s].astype(F32) + igr[s].astype(F32)).astype(BF16)
+
+    input_grad(6)
+    input_grad(2)
+    place_grad(1)
+    ip[2].recv()
+    core_sum(2)
+    ir_a = send(igc.at[2, 0:64], ia.at[0], dev(dz=1))
+    ir_b = send(igc.at[2, 64:128], ia.at[1], dev(dz=-1))
+    core_sum(3)
+    id_b = send(igc.at[3, 0:64], idr.at[0], dev(dz=-1))
+    place_grad(2)
+    input_grad(4)
+    input_grad(0)
+    stu_up()
+    stu_dn()
     relay(0)
-    lax.fori_loop(3, 4, input_grad, 0)
-    ip = send(igp.at[4:8], igr, dev(flip=True))
+    ip[0].recv()
+    core_sum(1)
+    id_a = send(igc.at[1, 64:128], idr.at[1], dev(dz=1))
+    core_sum(0)
     relay(1)
-    lax.fori_loop(0, 1, input_grad, 0)
     relay(2)
     spread(0)
-    lax.fori_loop(1, 2, input_grad, 0)
-    spread(1)
-    ip.recv()
-    for s in (2, 1, 3, 0):
-        igc[s] = (igp[s].astype(F32) + igr[s].astype(F32)).astype(BF16)
-        if s == 2:
-            ir_a = send(igc.at[2, 0:64], ia.at[0], dev(dz=1))
-            ir_b = send(igc.at[2, 64:128], ia.at[1], dev(dz=-1))
-        if s == 1:
-            id_a = send(igc.at[1, 64:128], idr.at[1], dev(dz=1))
-        if s == 3:
-            id_b = send(igc.at[3, 0:64], idr.at[0], dev(dz=-1))
-    spread(2)
 
     ir_a.recv()
     isum[0] = (ia[0].astype(F32) + igc[1, 0:64].astype(F32)).astype(BF16)
@@ -365,9 +417,11 @@
     isum[1] = (ia[1].astype(F32) + igc[3, 64:128].astype(F32)).astype(BF16)
     is_b = send(isum.at[1], idr.at[3], dev(dz=-1))
 
-    for c in ssent:
+    spread(1)
+    spread(2)
+    for c in stus.values():
         c.recv()
-    stu_out[...] = dot(rb[...], st[...], NT).astype(BF16)
+    stu_out[...] = dot(rb[...], st[...], (((0,), (1,)), ((), ()))).astype(BF16)
 
     total = ysend[:, :, blk(0)].astype(F32)
     for i in range(7):
@@ -401,7 +455,7 @@
             jax.ShapeDtypeStruct((128, 640), BF16),
             jax.ShapeDtypeStruct((9, 10, 80), F32),
         ),
-        in_specs=[vmem] * 3,
+        in_specs=[pl.BlockSpec(memory_space=pl.ANY)] * 3,
         out_specs=(vmem,) * 3,
         scratch_shapes=[
             pltpu.VMEM((4, 2, 80, 1024), BF16),
@@ -412,8 +466,9 @@
             pltpu.VMEM((1024, 128), BF16),
             pltpu.VMEM((8, 80, 128), BF16),
             pltpu.VMEM((2, 80, 128), BF16),
-            pltpu.VMEM((8, 128, 128), BF16),
-            pltpu.VMEM((128, 1024), BF16),
+            pltpu.VMEM((8, 80, 128), BF16),
+            pltpu.VMEM((2, 80, 128), BF16),
+            pltpu.VMEM((1024, 128), BF16),
             pltpu.VMEM((8, 192, 256), BF16),
             pltpu.VMEM((640, 768), F32),
             pltpu.VMEM((640, 768), BF16),
@@ -431,11 +486,14 @@
             pltpu.VMEM((2, 64, 640), BF16),
             pltpu.VMEM((2, 64, 640), BF16),
             pltpu.VMEM((4, 64, 640), BF16),
+            pltpu.VMEM((128, 640), BF16),
+            pltpu.VMEM((9, 10, 80), F32),
+            pltpu.SemaphoreType.DMA((3,)),
             pltpu.SemaphoreType.DMA((N_SEM,)),
             pltpu.SemaphoreType.DMA((N_SEM,)),
         ],
         compiler_params=pltpu.CompilerParams(
-            collective_id=0, has_side_effects=True, vmem_limit_bytes=48 << 20
+            collective_id=0, has_side_effects=True, vmem_limit_bytes=60600 << 10
         ),
     )(latents.reshape(128, 640), target.reshape(128, 640), weight.transpose(0, 2, 1))
     grad = grad.transpose(0, 2, 1)

time: 78.9 us -> 82.9 us (1.051)
  the two profiles are of different devices: /device:TPU:6 before, /device:TPU:1 now
where the time goes in v4:
time: 82.9 us; the launch traced here: 82.8 us
  Pallas kernels  78.8 us (95%)
  local copies, waits for them, and re-layouts  1.66 us (2%)
  other arithmetic  1.62 us (2%)
    pallas_call x1, Pallas kernels, per_device(): pl.pallas_call(kernel, out_shape=(jax.ShapeDtypeStruct((128, 640), BF16),...  78.8 us

profile of v4, /device:TPU:1, one launch (start us, length us, event | category | flops | bytes accessed | tf_op | source)
XLA Modules:
  0.0 82.8 jit_solution(6958944989967173528)
XLA Ops:
  0.6 0.0 copy-start
  0.6 0.0 copy-start.3
  0.7 0.0 copy-start.4
  0.7 78.8 %shard_map.92 = (bf16[128,640]{1,0:T(8,128)(2,1)}, bf16[128,640]{1,0:T(8,128)(2,1)}, f32[9,10,80]{2,1,0:T(8,128)}) custom-call(bf16[128,640]{1,0:T(8,128)(2,1)} %bitcast.13, bf16[128,640]{1,0:T(8,128)(2,1)} %bitcast.14, f32[9,10,80]{2,1,0:T(8,128)} %bitcast.12), custom_call_target="tpu_custom_call" | custom-call | tf_op jit(solution)/shard_map/pallas_call | solution.py:451
  79.5 0.0 copy-done
  79.5 0.0 copy-done.3
  79.5 0.0 copy-done.4
  79.5 0.0 copy-start.2
  79.5 1.6 %divide_subtract_fusion = (f32[9,80,10]{1,2,0:T(8,128)}, f32[9,80,10]{1,2,0:T(8,128)}, f32[9,80,10]{1,2,0:T(8,128)}) fusion(f32[9,80,10]{1,2,0:T(8,128)S(1)} %copy-done, f32[9,10,80]{2,1,0:T(8,128)} %get-tuple-element.10, f32[9,80,10]{1,2,0:T(8,128)S(1)} %copy-done.3, f32[9,80,10]{1,2,0:T(8,128)S(1)} %copy-done.4), kind=kLoop, calls=%fused_computation.4 | loop fusion | flops 79200 | bytes 201600 | tf_op jit(solution)/shard_map/sub | solution.py:502
  81.1 0.0 copy-done.2
  81.1 0.0 copy-start.1
  81.1 0.7 copy.12
  81.8 0.3 copy-done.1
  82.1 0.7 copy.13
Async XLA Ops:
  0.6 78.8 %copy-start = (f32[9,80,10]{1,2,0:T(8,128)S(1)}, f32[9,80,10]{1,2,0:T(8,128)}, u32[]{:S(2)}) copy-start(f32[9,80,10]{1,2,0:T(8,128)} %param.7) | copy-start | bytes 86404
  0.6 78.8 %copy-start.3 = (f32[9,80,10]{1,2,0:T(8,128)S(1)}, f32[9,80,10]{1,2,0:T(8,128)}, u32[]{:S(2)}) copy-start(f32[9,80,10]{1,2,0:T(8,128)} %param.8) | copy-start | bytes 86404
  0.7 78.8 %copy-start.4 = (f32[9,80,10]{1,2,0:T(8,128)S(1)}, f32[9,80,10]{1,2,0:T(8,128)}, u32[]{:S(2)}) copy-start(f32[9,80,10]{1,2,0:T(8,128)} %param.9) | copy-start | bytes 86404
  79.5 1.6 %copy-start.2 = (bf16[128,640]{1,0:T(8,128)(2,1)S(1)}, bf16[128,640]{1,0:T(8,128)(2,1)}, u32[]{:S(2)}) copy-start(bf16[128,640]{1,0:T(8,128)(2,1)} %get-tuple-element.8) | copy-start | bytes 491524
  81.1 1.0 %copy-start.1 = (bf16[128,640]{1,0:T(8,128)(2,1)S(1)}, bf16[128,640]{1,0:T(8,128)(2,1)}, u32[]{:S(2)}) copy-start(bf16[128,640]{1,0:T(8,128)(2,1)} %get-tuple-element.9) | copy-start | bytes 491524

commit v5 on v4

--- a/solution.py
+++ b/solution.py
@@ -11,7 +11,7 @@
 Y_ORDER = (1, 7, 2, 6, 3, 5, 4)
 BLOCKS = (4, 3, 5, 2, 6, 1, 7, 0)
 GROUPS = ((0, 384), (384, 640), (640, 1024))
-N_SEM = 160
+N_SEM = 125
 NT = (((1,), (1,)), ((), ()))
 TN = (((0,), (0,)), ((), ()))
 
@@ -38,7 +38,7 @@
 
 def kernel(
     lat_in, tgt_in, wgt_in, stu_out, ig_out, g_out,
-    kp, km, xs, st, sk, ts, tb, tr, sb, sr, rb, e3, gacc, gb, ga, ra, rs, rd, ysend, yr, zs, zr,
+    kp, km, xs, st, sk, ts, tb, tr, sb, sr, rb, eb, hb, e3, gacc, gb, ga, ra, rs, rd, ysend, yr, zs, zr,
     igp, igr, igc, ia, isum, idr, tgt, wgt, load_sem, send_sem, recv_sem,
 ):
     dp, row = lax.axis_index("dp"), lax.axis_index("rows")
@@ -86,8 +86,33 @@
     partners = [dev(flip_zl=True), dev(dx=1), dev(dx=-1), row_dev(1), row_dev(-1)]
     partners += [dev(dy=dy) for dy in Y_ORDER] + [dev(dz=dz) for dz in (1, 2, 3)]
     partners += [dev(dz=dz, flip=True) for dz in range(4)]
+    partners += [dev(dy=dy, flip_zl=True) for dy in (1, -1, 2, -2)]
     for partner in partners:
         pl.semaphore_signal(barrier, inc=1, device_id=partner, device_id_type=MESH)
+
+    loads[0].wait()
+    fill = jnp.zeros((6, 80), F32)
+    rows = jnp.concatenate([v for t in range(9) for v in (wgt[t], fill)], axis=0)
+    l9 = lax.broadcasted_iota(jnp.int32, (144, 128), 1)
+    n9 = lax.broadcasted_iota(jnp.int32, (144, 128), 0)
+    pick = (n9 & 15 < 10) & (l9 == (n9 >> 4) * 10 + (n9 & 15))
+    pick = jnp.where(pick, 1.0, 0.0).astype(BF16)
+    kp[0, 0, :, blk(0)] = dot(rows.astype(BF16), pick, TN).astype(BF16)
+    rb[...] = jnp.zeros((1024, 128), BF16)
+    loads[1].wait()
+    pl.semaphore_wait(barrier, len(partners))
+    p1, late = {}, {}
+    own = kp.at[0, 0, :, blk(0)]
+    for dy in (2, -2, 1, -1, 0):
+        for i in (1, 0) if dy else (1,):
+            p1[dy, i] = send(own, kp.at[0, i, :, blk(-dy)], dev(dy=dy, flip_zl=i == 1))
+    top = [send(lat.at[0:32], xs.at[0, 160:192], row_dev(-1))]
+    bot = [send(lat.at[96:128], xs.at[0, 0:32], row_dev(1))]
+    up0 = send(lat.at[0:64], xs.at[3, 32:96], dev(dz=1))
+    dn1 = send(lat.at[64:128], xs.at[1, 96:160], dev(dz=-1))
+    up1 = send(lat.at[64:128], xs.at[3, 96:160], dev(dz=1))
+    dn0 = send(lat.at[0:64], xs.at[1, 32:96], dev(dz=-1))
+    part = {0: send(lat, xs.at[4, 32:160], dev(flip=True))}
 
     lane = lax.broadcasted_iota(jnp.int32, (640, 128), 1)
     chan = lax.broadcasted_iota(jnp.int32, (640, 128), 0)
@@ -107,37 +132,10 @@
         hit = jnp.where(diff == (y + dy) % 8 * 10, 1.0, 0.0)
         sk[j * 128 : j * 128 + 128, :] = hit.astype(BF16)
 
-    loads[0].wait()
-    fill = jnp.zeros((6, 80), F32)
-    rows = jnp.concatenate([v for t in range(9) for v in (wgt[t], fill)], axis=0)
-    l9 = lax.broadcasted_iota(jnp.int32, (144, 128), 1)
-    n9 = lax.broadcasted_iota(jnp.int32, (144, 128), 0)
-    pick = (n9 & 15 < 10) & (l9 == (n9 >> 4) * 10 + (n9 & 15))
-    pick = jnp.where(pick, 1.0, 0.0).astype(BF16)
-    kp[0, 0, :, blk(0)] = dot(rows.astype(BF16), pick, TN).astype(BF16)
-    rb[...] = jnp.zeros((1024, 128), BF16)
     loads[2].wait()
     ts[...] = dot(st[...], tgt[...], (((0,), (1,)), ((), ()))).astype(BF16)
     tb[0] = ts[0:80]
-    loads[1].wait()
-    pl.semaphore_wait(barrier, len(partners))
-    p0 = send(kp.at[0, 0, :, blk(0)], kp.at[0, 1, :, blk(0)], dev(flip_zl=True))
-    up0 = send(lat.at[0:64], xs.at[3, 32:96], dev(dz=1))
-    dn1 = send(lat.at[64:128], xs.at[1, 96:160], dev(dz=-1))
-    up1 = send(lat.at[64:128], xs.at[3, 96:160], dev(dz=1))
-    dn0 = send(lat.at[0:64], xs.at[1, 32:96], dev(dz=-1))
-    part = {0: send(lat, xs.at[4, 32:160], dev(flip=True))}
-    top = [send(lat.at[0:32], xs.at[0, 160:192], row_dev(-1))]
-    bot = [send(lat.at[96:128], xs.at[0, 0:32], row_dev(1))]
-
-    p0.recv()
-    block = kp.at[0, :, :, blk(0)]
-    p1, late = {}, {}
-    for dy in (2, -2, 1, -1):
-        p1[dy] = send(block, kp.at[0, :, :, blk(-dy)], dev(dy=dy))
     right, left, fwd_r, fwd_l = {}, {}, {}, {}
-    right[0] = send(block, kp.at[3, :, :, blk(0)], dev(dx=1))
-    left[0] = send(block, kp.at[1, :, :, blk(0)], dev(dx=-1))
 
     halo = {0: (top[0], bot[0])}
 
@@ -153,14 +151,23 @@
         left[dy] = send(got, kp.at[1, :, :, blk(-dy)], dev(dx=-1))
 
     def y_near(dy):
-        p1[dy].recv()
+        p1[dy, 1].recv()
+        p1[dy, 0].recv()
         if dy in (2, -2):
             one, half = dy // 2, 0 if dy > 0 else 1
-            got = kp.at[0, :, :, blk(-dy)]
-            p1[dy + one] = send(got, kp.at[0, :, :, blk(-dy - one)], dev(dy=one))
             dst = kp.at[0, half, :, blk(4)]
             late[half] = send(kp.at[0, half, :, blk(-dy)], dst, dev(dy=dy))
+            got = kp.at[0, :, :, blk(-dy)]
+            late[dy + one] = send(got, kp.at[0, :, :, blk(-dy - one)], dev(dy=one))
         x_sends(dy)
+
+    ends = {}
+
+    def edges(s):
+        ends[s] = []
+        for c, edge in zip(halo[s], (slice(160, 192), slice(0, 32))):
+            c.recv()
+            ends[s].append(send(xs.at[s, edge], xs.at[s + 4, edge], dev(flip=True)))
 
     def x_step(dy):
         right[dy].recv()
@@ -188,6 +195,8 @@
 
         return sent, relay_up, relay_dn
 
+    p1[0, 1].recv()
+    x_sends(0)
     y_near(2)
     y_near(-2)
     y_near(1)
@@ -197,13 +206,11 @@
     over0 = send(xs.at[3, 32:96], xs.at[2, 32:96], dev(dz=1))
     dn1.recv()
     over1 = send(xs.at[1, 96:160], xs.at[2, 96:160], dev(dz=-1))
-    goals, goal_up, goal_dn = to_group(
-        lambda s: ts.at[s * 128 : s * 128 + 80], lambda s: tb.at[s], tr
-    )
     x_step(2)
     x_step(-2)
-    y_near(3)
-    y_near(-3)
+    for dy in (3, -3):
+        late[dy].recv()
+        x_sends(dy)
     late[0].recv()
     late[1].recv()
     x_sends(4)
@@ -213,9 +220,18 @@
     halos(3)
     dn0.recv()
     halos(1)
+    goals, goal_up, goal_dn = to_group(
+        lambda s: ts.at[s * 128 : s * 128 + 80], lambda s: tb.at[s], tr
+    )
     x_step(3)
     x_step(-3)
+    over0.recv()
+    over1.recv()
+    halos(2)
     x_step(4)
+    edges(0)
+    edges(3)
+    edges(1)
 
     def place_kernel(dx):
         out = dot(kp[dx].reshape(160, 1024), sk[...]).astype(BF16)
@@ -223,14 +239,12 @@
         km[rows_of(dx, 1), :] = out[80:]
 
     place_kernel(0)
+    edges(2)
+    goal_up()
+    goal_dn()
     place_kernel(1)
     place_kernel(3)
 
-    over0.recv()
-    over1.recv()
-    halos(2)
-    goal_up()
-    goal_dn()
     for dy in range(8):
         dy = dy if dy < 5 else dy - 8
         fwd_r[dy].recv()
@@ -242,12 +256,8 @@
     real = lax.broadcasted_iota(jnp.int32, (256, 128), 1) < 80
 
     def pair_ready(s):
-        ends = []
-        for c, edge in zip(halo[s], (slice(160, 192), slice(0, 32))):
-            c.recv()
-            ends.append(send(xs.at[s, edge], xs.at[s + 4, edge], dev(flip=True)))
         part[s].recv()
-        for c in ends:
+        for c in ends[s]:
             c.recv()
             c.sent()
 
@@ -267,6 +277,15 @@
 
     def joined(ref, s, rows):
         return jnp.concatenate([ref[s, rows], ref[s + 4, rows]], axis=0)
+
+    def widened(err):
+        zero = jnp.zeros((256, 128), F32)
+        nxt = jnp.where(last, 0.0, pltpu.roll(err, 255, 0))
+        prv = jnp.where(first, 0.0, pltpu.roll(err, 1, 0))
+        wide = jnp.concatenate([nxt, zero], axis=1)
+        wide = wide + pltpu.roll(jnp.concatenate([err, zero], axis=1), 80, 1)
+        wide = wide + pltpu.roll(jnp.concatenate([prv, zero], axis=1), 160, 1)
+        return wide.astype(BF16)
 
     def forward(s):
         acc = None
@@ -287,22 +306,18 @@
             goal.append(jnp.concatenate([tb[at].astype(F32), fill], axis=0).T)
         err = stu - jnp.concatenate(goal, axis=0)
         err = err.astype(BF16).astype(F32)
-        zero = jnp.zeros((256, 128), F32)
-        nxt = jnp.where(last, 0.0, pltpu.roll(err, 255, 0))
-        prv = jnp.where(first, 0.0, pltpu.roll(err, 1, 0))
-        wide = jnp.concatenate([nxt, zero], axis=1)
-        wide = wide + pltpu.roll(jnp.concatenate([err, zero], axis=1), 80, 1)
-        wide = wide + pltpu.roll(jnp.concatenate([prv, zero], axis=1), 160, 1)
-        wide = wide.astype(BF16)
+        for i, at in enumerate((s, s + 4)):
+            eb[at] = err[128 * i : 128 * i + 128].astype(BF16)
+        wide = widened(err)
         e3[s, 32:160, :] = wide[:128]
         e3[s + 4, 32:160, :] = wide[128:]
 
+    err_halos = []
     for s in (0, 3, 1, 2):
         pair_ready(s)
         forward(s)
-
-    etop = send(e3.at[:, 32:64], e3.at[:, 160:192], row_dev(-1))
-    ebot = send(e3.at[:, 128:160], e3.at[:, 0:32], row_dev(1))
+    err_halos.append(send(eb.at[:, 0:32], hb.at[1], row_dev(-1)))
+    err_halos.append(send(eb.at[:, 96:128], hb.at[0], row_dev(1)))
     stus, stu_up, stu_dn = to_group(
         lambda s: sb.at[s], lambda s: rb.at[s * 128 : s * 128 + 80], sr
     )
@@ -354,15 +369,18 @@
             mine = ga[rows_of(0, i), cols].astype(F32)
             both = rd[i, :, cols].astype(F32) + rd[i + 2, :, cols].astype(F32)
             ysend[i, :, cols] = (mine + both).astype(BF16)
-        for dy in BLOCKS[GROUPS[g][0] // 128 : GROUPS[g][1] // 128]:
+        for dy in BLOCKS[cols.start // 128 : cols.stop // 128]:
             if dy:
                 ysent.append(send(ysend.at[:, :, blk(dy)], yr.at[len(ysent)], dev(dy=dy)))
 
     place_grad(0)
-    etop.recv()
-    ebot.recv()
-    etop.sent()
-    ebot.sent()
+    place_grad(1)
+    place_grad(2)
+    for c in err_halos:
+        c.recv()
+    for i, edge in enumerate((slice(0, 32), slice(160, 192))):
+        wide = widened(hb[i].reshape(256, 128).astype(F32))
+        e3[:, edge, :] = wide.reshape(8, 32, 256)
 
     @pl.when(row == 0)
     def _():
@@ -389,19 +407,17 @@
 
     input_grad(6)
     input_grad(2)
-    place_grad(1)
     ip[2].recv()
     core_sum(2)
     ir_a = send(igc.at[2, 0:64], ia.at[0], dev(dz=1))
     ir_b = send(igc.at[2, 64:128], ia.at[1], dev(dz=-1))
     core_sum(3)
     id_b = send(igc.at[3, 0:64], idr.at[0], dev(dz=-1))
-    place_grad(2)
-    input_grad(4)
-    input_grad(0)
     stu_up()
     stu_dn()
+    input_grad(4)
     relay(0)
+    input_grad(0)
     ip[0].recv()
     core_sum(1)
     id_a = send(igc.at[1, 64:128], idr.at[1], dev(dz=1))
@@ -409,6 +425,7 @@
     relay(1)
     relay(2)
     spread(0)
+    spread(1)
 
     ir_a.recv()
     isum[0] = (ia[0].astype(F32) + igc[1, 0:64].astype(F32)).astype(BF16)
@@ -417,18 +434,17 @@
     isum[1] = (ia[1].astype(F32) + igc[3, 64:128].astype(F32)).astype(BF16)
     is_b = send(isum.at[1], idr.at[3], dev(dz=-1))
 
-    spread(1)
     spread(2)
-    for c in stus.values():
-        c.recv()
-    stu_out[...] = dot(rb[...], st[...], (((0,), (1,)), ((), ()))).astype(BF16)
-
     total = ysend[:, :, blk(0)].astype(F32)
     for i in range(7):
         ysent[i].recv()
         total = total + yr[i].astype(F32)
     zs[...] = total
     zc = send(zs.at[1], zr, dev(flip_zl=True))
+    for c in stus.values():
+        c.recv()
+    stu_out[...] = dot(rb[...], st[...], (((0,), (1,)), ((), ()))).astype(BF16)
+
 
     for c in (id_a, id_b, is_a, is_b):
         c.recv()
@@ -438,7 +454,8 @@
     ig_out[64:128] = high.astype(BF16)
 
     zc.recv()
-    grad = (zs[0] + zr[...]) * (1.0 / 64.0)
+    total = zs[0] + zr[...]
+    grad = total * (1.0 / 64.0)
     turned = jnp.concatenate([grad, jnp.zeros((48, 128), F32)], axis=0).T
     for t in range(9):
         g_out[t] = turned[10 * t : 10 * t + 10, :80]
@@ -469,6 +486,8 @@
             pltpu.VMEM((8, 80, 128), BF16),
             pltpu.VMEM((2, 80, 128), BF16),
             pltpu.VMEM((1024, 128), BF16),
+            pltpu.VMEM((8, 128, 128), BF16),
+            pltpu.VMEM((2, 8, 32, 128), BF16),
             pltpu.VMEM((8, 192, 256), BF16),
             pltpu.VMEM((640, 768), F32),
             pltpu.VMEM((640, 768), BF16),
@@ -493,7 +512,7 @@
             pltpu.SemaphoreType.DMA((N_SEM,)),
         ],
         compiler_params=pltpu.CompilerParams(
-            collective_id=0, has_side_effects=True, vmem_limit_bytes=60600 << 10
+            collective_id=0, has_side_effects=True, vmem_limit_bytes=48 << 20
         ),
     )(latents.reshape(128, 640), target.reshape(128, 640), weight.transpose(0, 2, 1))
     grad = grad.transpose(0, 2, 1)

time: 82.9 us -> 76.9 us (0.928)
  Pallas kernels: 78.8 us -> 71.2 us
  local copies, waits for them, and re-layouts: 1.66 us -> 4.05 us
  other arithmetic: 1.62 us -> 0.7 us
    pallas_call x1, Pallas kernels: 78.8 us -> 71.2 us  [per_device(): pl.pallas_call(kernel, out_shape=(jax.ShapeDtypeStruct((128, 640), BF16),...]
    unnamed x12, local copies, waits for them, and re-layouts: 1.66 us -> 4.05 us
    sub x1, other arithmetic: 1.62 us -> 0.7 us  [per_device(): new_weight = weight - 0.01 * new_moment1 / (jnp.sqrt(new_moment2) + 1e-08)]
where the time goes in v5:
time: 76.9 us; the launch traced here: 76.7 us
  Pallas kernels  71.2 us (93%)
  local copies, waits for them, and re-layouts  4.05 us (5%)
    pallas_call x1, Pallas kernels, per_device(): pl.pallas_call(kernel, out_shape=(jax.ShapeDtypeStruct((128, 640), BF16),...  71.2 us
    unnamed x12, local copies, waits for them, and re-layouts  4.05 us

profile of v5, /device:TPU:1, one launch (start us, length us, event | category | flops | bytes accessed | tf_op | source)
XLA Modules:
  0.0 76.7 jit_solution(15824828876742804425)
XLA Ops:
  0.6 0.0 copy-start
  0.6 0.9 %copy-done = f32[9,80,10]{1,2,0:T(8,128)S(1)} copy-done((f32[9,80,10]{1,2,0:T(8,128)S(1)}, f32[9,80,10]{1,2,0:T(8,128)}, u32[]{:S(2)}) %copy-start) | copy-done | bytes 28824
  1.5 0.0 copy-start.1
  1.5 0.9 %copy-done.1 = bf16[1,4,32,640]{3,2,1,0:T(8,128)(2,1)S(1)} copy-done((bf16[1,4,32,640]{3,2,1,0:T(8,128)(2,1)S(1)}, bf16[1,4,32,640]{3,2,1,0:T(8,128)(2,1)}, u32[]{:S(2)}) %copy-start.1) | copy-done | bytes 163864
  2.4 0.0 copy-start.2
  2.4 0.9 %copy-done.2 = bf16[1,4,32,640]{3,2,1,0:T(8,128)(2,1)S(1)} copy-done((bf16[1,4,32,640]{3,2,1,0:T(8,128)(2,1)S(1)}, bf16[1,4,32,640]{3,2,1,0:T(8,128)(2,1)}, u32[]{:S(2)}) %copy-start.2) | copy-done | bytes 163864
  3.4 0.0 copy-start.3
  3.4 0.0 copy-start.4
  3.4 71.2 %shard_map.92 = (bf16[128,640]{1,0:T(8,128)(2,1)S(1)}, bf16[128,640]{1,0:T(8,128)(2,1)S(1)}, f32[9,10,80]{2,1,0:T(8,128)S(1)}) custom-call(bf16[128,640]{1,0:T(8,128)(2,1)S(1)} %bitcast.13, bf16[128,640]{1,0:T(8,128)(2,1)S(1)} %bitcast.14, f32[9,10,80]{2,1,0:T(8,128)S(1)} %bitcast.12), custom_call_target="tpu_custom_call" | custom-call | tf_op jit(solution)/shard_map/pallas_call | solution.py:468
  74.6 0.0 copy-done.3
  74.6 0.0 copy-done.4
  74.6 0.7 divide_subtract_fusion
  75.3 0.7 copy.12
  76.0 0.7 copy.13
Async XLA Ops:
  0.6 0.9 %copy-start = (f32[9,80,10]{1,2,0:T(8,128)S(1)}, f32[9,80,10]{1,2,0:T(8,128)}, u32[]{:S(2)}) copy-start(f32[9,80,10]{1,2,0:T(8,128)} %param.7) | copy-start | bytes 86404
  1.5 0.9 %copy-start.1 = (bf16[1,4,32,640]{3,2,1,0:T(8,128)(2,1)S(1)}, bf16[1,4,32,640]{3,2,1,0:T(8,128)(2,1)}, u32[]{:S(2)}) copy-start(bf16[1,4,32,640]{3,2,1,0:T(8,128)(2,1)} %param.5) | copy-start | bytes 491524
  2.4 0.9 %copy-start.2 = (bf16[1,4,32,640]{3,2,1,0:T(8,128)(2,1)S(1)}, bf16[1,4,32,640]{3,2,1,0:T(8,128)(2,1)}, u32[]{:S(2)}) copy-start(bf16[1,4,32,640]{3,2,1,0:T(8,128)(2,1)} %param.6) | copy-start | bytes 491524
  3.4 71.3 %copy-start.3 = (f32[9,80,10]{1,2,0:T(8,128)S(1)}, f32[9,80,10]{1,2,0:T(8,128)}, u32[]{:S(2)}) copy-start(f32[9,80,10]{1,2,0:T(8,128)} %param.8) | copy-start | bytes 86404
  3.4 71.3 %copy-start.4 = (f32[9,80,10]{1,2,0:T(8,128)S(1)}, f32[9,80,10]{1,2,0:T(8,128)}, u32[]{:S(2)}) copy-start(f32[9,80,10]{1,2,0:T(8,128)} %param.9) | copy-start | bytes 86404

commit v6 on v5

--- a/solution.py
+++ b/solution.py
@@ -38,7 +38,7 @@
 
 def kernel(
     lat_in, tgt_in, wgt_in, stu_out, ig_out, g_out,
-    kp, km, xs, st, sk, ts, tb, tr, sb, sr, rb, eb, hb, e3, gacc, gb, ga, ra, rs, rd, ysend, yr, zs, zr,
+    kp, km, xs, st, sk, ts, tb, tr, sn, sb, sr, rb, eb, hb, e3, gacc, gb, ga, ra, rs, rd, ysend, yr, zs, zr,
     igp, igr, igc, ia, isum, idr, tgt, wgt, load_sem, send_sem, recv_sem,
 ):
     dp, row = lax.axis_index("dp"), lax.axis_index("rows")
@@ -301,7 +301,7 @@
         stu = stu.astype(F32)
         goal = []
         for i, at in enumerate((s, s + 4)):
-            sb[at] = stu[128 * i : 128 * i + 128].T[:80].astype(BF16)
+            sn[at] = stu[128 * i : 128 * i + 128].astype(BF16)
             fill = jnp.zeros((48, 128), F32)
             goal.append(jnp.concatenate([tb[at].astype(F32), fill], axis=0).T)
         err = stu - jnp.concatenate(goal, axis=0)
@@ -318,11 +318,6 @@
         forward(s)
     err_halos.append(send(eb.at[:, 0:32], hb.at[1], row_dev(-1)))
     err_halos.append(send(eb.at[:, 96:128], hb.at[0], row_dev(1)))
-    stus, stu_up, stu_dn = to_group(
-        lambda s: sb.at[s], lambda s: rb.at[s * 128 : s * 128 + 80], sr
-    )
-    rb[0:80] = sb[0]
-
     gacc[...] = jnp.zeros((640, 768), F32)
 
     def weight_grad(m, carry):
@@ -376,6 +371,12 @@
     place_grad(0)
     place_grad(1)
     place_grad(2)
+    for s in range(8):
+        sb[s] = sn[s].astype(F32).T[:80].astype(BF16)
+    stus, stu_up, stu_dn = to_group(
+        lambda s: sb.at[s], lambda s: rb.at[s * 128 : s * 128 + 80], sr
+    )
+    rb[0:80] = sb[0]
     for c in err_halos:
         c.recv()
     for i, edge in enumerate((slice(0, 32), slice(160, 192))):
@@ -483,6 +484,7 @@
             pltpu.VMEM((1024, 128), BF16),
             pltpu.VMEM((8, 80, 128), BF16),
             pltpu.VMEM((2, 80, 128), BF16),
+            pltpu.VMEM((8, 128, 128), BF16),
             pltpu.VMEM((8, 80, 128), BF16),
             pltpu.VMEM((2, 80, 128), BF16),
             pltpu.VMEM((1024, 128), BF16),

time: 76.9 us -> 77.6 us (level)
  Pallas kernels: 71.2 us -> 72 us
where the time goes in v6:
time: 77.6 us; the launch traced here: 77.4 us
  Pallas kernels  72 us (93%)
  local copies, waits for them, and re-layouts  4.05 us (5%)
    pallas_call x1, Pallas kernels, per_device(): pl.pallas_call(kernel, out_shape=(jax.ShapeDtypeStruct((128, 640), BF16),...  72 us
    unnamed x12, local copies, waits for them, and re-layouts  4.05 us

profile of v6, /device:TPU:1, one launch (start us, length us, event | category | flops | bytes accessed | tf_op | source)
XLA Modules:
  0.0 77.4 jit_solution(8415902569710741672)
XLA Ops:
  0.6 0.0 copy-start
  0.6 0.9 %copy-done = f32[9,80,10]{1,2,0:T(8,128)S(1)} copy-done((f32[9,80,10]{1,2,0:T(8,128)S(1)}, f32[9,80,10]{1,2,0:T(8,128)}, u32[]{:S(2)}) %copy-start) | copy-done | bytes 28824
  1.5 0.0 copy-start.1
  1.5 0.9 %copy-done.1 = bf16[1,4,32,640]{3,2,1,0:T(8,128)(2,1)S(1)} copy-done((bf16[1,4,32,640]{3,2,1,0:T(8,128)(2,1)S(1)}, bf16[1,4,32,640]{3,2,1,0:T(8,128)(2,1)}, u32[]{:S(2)}) %copy-start.1) | copy-done | bytes 163864
  2.4 0.0 copy-start.2
  2.4 0.9 %copy-done.2 = bf16[1,4,32,640]{3,2,1,0:T(8,128)(2,1)S(1)} copy-done((bf16[1,4,32,640]{3,2,1,0:T(8,128)(2,1)S(1)}, bf16[1,4,32,640]{3,2,1,0:T(8,128)(2,1)}, u32[]{:S(2)}) %copy-start.2) | copy-done | bytes 163864
  3.4 0.0 copy-start.3
  3.4 0.0 copy-start.4
  3.4 72.0 %shard_map.92 = (bf16[128,640]{1,0:T(8,128)(2,1)S(1)}, bf16[128,640]{1,0:T(8,128)(2,1)S(1)}, f32[9,10,80]{2,1,0:T(8,128)S(1)}) custom-call(bf16[128,640]{1,0:T(8,128)(2,1)S(1)} %bitcast.13, bf16[128,640]{1,0:T(8,128)(2,1)S(1)} %bitcast.14, f32[9,10,80]{2,1,0:T(8,128)S(1)} %bitcast.12), custom_call_target="tpu_custom_call" | custom-call | tf_op jit(solution)/shard_map/pallas_call | solution.py:469
  75.3 0.0 copy-done.3
  75.4 0.0 copy-done.4
  75.4 0.7 divide_subtract_fusion
  76.1 0.7 copy.12
  76.7 0.7 copy.13
Async XLA Ops:
  0.6 0.9 %copy-start = (f32[9,80,10]{1,2,0:T(8,128)S(1)}, f32[9,80,10]{1,2,0:T(8,128)}, u32[]{:S(2)}) copy-start(f32[9,80,10]{1,2,0:T(8,128)} %param.7) | copy-start | bytes 86404
  1.5 0.9 %copy-start.1 = (bf16[1,4,32,640]{3,2,1,0:T(8,128)(2,1)S(1)}, bf16[1,4,32,640]{3,2,1,0:T(8,128)(2,1)}, u32[]{:S(2)}) copy-start(bf16[1,4,32,640]{3,2,1,0:T(8,128)(2,1)} %param.5) | copy-start | bytes 491524
  2.4 0.9 %copy-start.2 = (bf16[1,4,32,640]{3,2,1,0:T(8,128)(2,1)S(1)}, bf16[1,4,32,640]{3,2,1,0:T(8,128)(2,1)}, u32[]{:S(2)}) copy-start(bf16[1,4,32,640]{3,2,1,0:T(8,128)(2,1)} %param.6) | copy-start | bytes 491524
  3.4 72.0 %copy-start.3 = (f32[9,80,10]{1,2,0:T(8,128)S(1)}, f32[9,80,10]{1,2,0:T(8,128)}, u32[]{:S(2)}) copy-start(f32[9,80,10]{1,2,0:T(8,128)} %param.8) | copy-start | bytes 86404
  3.4 72.0 %copy-start.4 = (f32[9,80,10]{1,2,0:T(8,128)S(1)}, f32[9,80,10]{1,2,0:T(8,128)}, u32[]{:S(2)}) copy-start(f32[9,80,10]{1,2,0:T(8,128)} %param.9) | copy-start | bytes 86404
